TPU v7x, 32 devices: a whole 2x2x4 slice. The times are simulated.
32 devices in a mesh: parts: 2 (over y), cand: 4 (over z), query: 4 (over x, core).
Axes of the slice: x: 2, y: 2, z: 4, core: 2. Of those that a mesh axis runs over, the one named last changes fastest.
Arguments:
- cand_out: bfloat16 [24, 4, 5120], P(('parts', 'cand')), parts along dimension 0, may hold values from -6 to 6
- cand_in: bfloat16 [24, 4, 13824], P(('parts', 'cand')), parts along dimension 0, may hold values from -6 to 6
- query_out: bfloat16 [32, 8, 5120], P(('parts', 'query')), parts along dimension 0, may hold values from -0.03125 to 0.03125
- query_in: bfloat16 [32, 8, 13824], P(('parts', 'query')), parts along dimension 0, may hold values from -0.02734375 to 0.02734375
- eigenvalues: bfloat16 [4, 2560, 6912], P('cand'), may hold values from 0.19921875 to 5
- slot_blocks: int32 [8, 4, 2], P(('parts', 'query')), parts along dimension 0, may hold values from 0 to 2, as said below
- live_counts: int32 [8, 4], P(('parts', 'query')), parts along dimension 0, may hold values from 1 to 2, as said below
Outputs:
- scores: float32 [32, 4, 2], P(('parts', 'query'), 'cand'), parts along dimension 0
There are 2 independent parts, one for each index of `parts`. A program takes and returns all parts, laid end to end along the dimension named above; an argument that names none is the same for every part. Nothing has to cross between parts.
Inputs may be any that keep to these rules, and one draw needn't show every extreme that they name: slot_blocks[g, k] holds 2 distinct blocks of the 3 blocks of source k. `live_counts`: every group has a source whose 2 slots are all used.
All inputs are finite; a program needn't handle non-finite values.
Results may differ from a plain program's by a relative error of at most 0.0029.
Values may be sent and summed in bfloat16 or wider, within the bound.
No kernel may reach another device: no remote copies, remote signals or barrier semaphores. Data moves between devices by JAX's collectives and lax.ppermute only.
A program may use at most 192 MiB of HBM per device.

v0:
```python
import jax
import jax.numpy as jnp
from jax import lax
from jax.sharding import PartitionSpec as P

DAMPING = 0.05


def tile_pieces(outside, inside, row_tiles, col_tiles):
    block_count, tokens, width_out = outside.shape
    row_width = width_out // row_tiles
    col_width = inside.shape[2] // col_tiles
    out_parts = jnp.moveaxis(outside.reshape(block_count, tokens, row_tiles, row_width), 2, 0)
    out_parts = jnp.broadcast_to(
        out_parts[:, None], (row_tiles, col_tiles, block_count, tokens, row_width)
    )
    out_parts = out_parts.reshape(row_tiles * col_tiles, block_count, tokens, row_width)
    in_parts = jnp.moveaxis(inside.reshape(block_count, tokens, col_tiles, col_width), 2, 0)
    in_parts = jnp.broadcast_to(
        in_parts[None], (row_tiles, col_tiles, block_count, tokens, col_width)
    )
    in_parts = in_parts.reshape(row_tiles * col_tiles, block_count, tokens, col_width)
    return (out_parts, in_parts)


def block_scores(precond, out_parts, in_parts):
    sources, block_count, tokens, row_width = out_parts.shape
    col_width = in_parts.shape[3]
    flat_in = in_parts.reshape(sources * block_count * tokens, col_width)
    flat_out = out_parts.reshape(sources * block_count * tokens, row_width)
    mapped = jnp.einsum("qij,nj->qin", precond, flat_in, preferred_element_type=jnp.float32)
    summed = jnp.sum(mapped * flat_out.T.astype(jnp.float32)[None], axis=1)
    return summed.reshape(precond.shape[0], sources, block_count, tokens).sum(axis=3)


def body(cand_out, cand_in, query_out, query_in, eigenvalues, slot_blocks, live_counts):
    tile_count = lax.axis_size("cand")
    row_tiles = min(8, max(2, tile_count // 8))
    col_tiles = tile_count // row_tiles
    position = lax.axis_index("cand")
    row_part = position // col_tiles
    col_part = position % col_tiles
    row_width = cand_out.shape[2] // row_tiles
    col_width = cand_in.shape[2] // col_tiles
    out_factor = lax.dynamic_slice_in_dim(query_out, row_part * row_width, row_width, 2)
    in_factor = lax.dynamic_slice_in_dim(query_in, col_part * col_width, col_width, 2)
    outer_sum = jnp.einsum(
        "qri,qrj->qij", out_factor, in_factor, preferred_element_type=jnp.float32
    )
    precond = (outer_sum / (eigenvalues[0].astype(jnp.float32) + DAMPING)).astype(jnp.bfloat16)
    group_slots = slot_blocks[0]
    slot_count = group_slots.shape[1]
    live_slots = (
        jnp.arange(slot_count, dtype=jnp.int32)[None, :] < live_counts[0][:, None]
    ).astype(jnp.float32)
    own_slots = lax.dynamic_index_in_dim(group_slots, position, 0, keepdims=False)
    own_live = lax.dynamic_index_in_dim(live_slots, position, 0, keepdims=False)
    live_mask = own_live.astype(jnp.bfloat16)[:, None, None]
    chosen_out = jnp.take(cand_out, own_slots, axis=0) * live_mask
    chosen_in = jnp.take(cand_in, own_slots, axis=0) * live_mask
    out_parts, in_parts = tile_pieces(chosen_out, chosen_in, row_tiles, col_tiles)
    partial_value = block_scores(
        precond,
        lax.all_to_all(out_parts, "cand", split_axis=0, concat_axis=0, tiled=True),
        lax.all_to_all(in_parts, "cand", split_axis=0, concat_axis=0, tiled=True),
    )
    totals = lax.psum_scatter(partial_value, "cand", scatter_dimension=1, tiled=True)
    return totals


def solution(mesh):
    return jax.shard_map(
        body,
        mesh=mesh,
        in_specs=(
            P(("parts", "cand"), None, None),
            P(("parts", "cand"), None, None),
            P(("parts", "query"), None, None),
            P(("parts", "query"), None, None),
            P("cand", None, None),
            P(("parts", "query"), None, None),
            P(("parts", "query"), None),
        ),
        out_specs=P(("parts", "query"), "cand", None),
        check_vma=False,
    )
```

profile of v0, /device:TPU:0, one launch (start us, length us, event | category | flops | bytes accessed | tf_op | source)
XLA Modules:
  0.0 153.4 jit_solution(16645560817307960975)
XLA Ops:
  0.0 0.0 copy-start
  0.0 0.0 copy-start.2
  0.0 0.0 copy-start.1
  0.0 1.0 dynamic-slice_reduce_fusion
  1.0 0.7 fusion.7
  1.7 1.5 gather_fusion.1
  3.3 0.2 multiply_bitcast_fusion.1
  3.5 0.7 broadcast_in_dim.41
  4.2 6.4 %all-to-all-start.1 = ((bf16[4,2,4,2560]{3,2,1,0:T(4,128)(2,1)}), bf16[4,2,4,2560]{3,2,1,0:T(4,128)(2,1)S(1)}, u32[]{:S(2)}, u32[]{:S(2)}) async-start(bf16[4,2,4,2560]{3,2,1,0:T(4,128)(2,1)} %bitcast.7), calls=%async_computation.1 | async-start | bytes 327680 | tf_op jit(solution)/shard_map/all_to_all | solution.py:64
  10.6 1.7 %gather_fusion = bf16[2,4,13824]{2,1,0:T(4,128)(2,1)S(1)} fusion(bf16[3,4,13824]{2,1,0:T(4,128)(2,1)} %param.8, s32[1024]{0:T(1024)S(1)} %pad_clamp_fusion), kind=kCustom, calls=%fused_computation | custom fusion | bytes 442376 | tf_op jit(solution)/shard_map/jit(_take)/gather | solution.py:60
  12.3 0.1 gather.13
  12.4 0.3 multiply_bitcast_fusion
  12.7 0.1 copy.10
  12.8 4.2 %all-to-all-done.1 = bf16[4,2,4,2560]{3,2,1,0:T(4,128)(2,1)S(1)} async-done(((bf16[4,2,4,2560]{3,2,1,0:T(4,128)(2,1)}), bf16[4,2,4,2560]{3,2,1,0:T(4,128)(2,1)S(1)}, u32[]{:S(2)}, u32[]{:S(2)}) %all-to-all-start.1) | async-done | bytes 163872 | tf_op jit(solution)/shard_map/all_to_all | solution.py:64
  17.0 0.9 broadcast_in_dim.38
  17.9 3.5 %all-to-all-start = ((bf16[4,2,4,6912]{3,2,1,0:T(4,128)(2,1)}), bf16[4,2,4,6912]{3,2,1,0:T(4,128)(2,1)S(1)}, u32[]{:S(2)}, u32[]{:S(2)}) async-start(bf16[4,2,4,6912]{3,2,1,0:T(4,128)(2,1)} %bitcast.5), calls=%async_computation | async-start | bytes 884736 | tf_op jit(solution)/shard_map/all_to_all | solution.py:65
  21.3 34.6 %add_bitcast_fusion = f32[2560,6912]{1,0:T(8,128)} fusion(bf16[1,2560,6912]{2,1,0:T(8,128)(2,1)} %param.11), kind=kLoop, calls=%fused_computation.3 | loop fusion | flops 35389440 | bytes 106168320 | tf_op jit(solution)/shard_map/div | solution.py:50
  55.9 0.0 copy-done.2
  55.9 0.6 dynamic-slice.1
  56.5 0.0 all-to-all-done
  56.5 0.1 reshape.86
  56.6 0.0 copy-done
  56.6 0.0 copy-done.1
  56.6 83.2 %fusion.2 = f32[4,32]{1,0:T(4,128)S(1)} fusion(bf16[32,6912,1]{1,0,2:T(8,128)(2,1)S(1)} %reshape.86, f32[2560,6912]{1,0:T(8,128)} %add_bitcast_fusion, f32[2560,32]{0,1:T(8,128)S(1)} %bitcast.19, bf16[4,8,13824]{2,1,0:T(8,128)(2,1)S(1)} %copy-done, s32[]{:T(128)S(6)} %select_n.54, bf16[4,8,5120]{2,1,0:T(8,128)(2,1)S(1)} %copy-done.1, s32[]{:T(128)S(6)} %select_n.52), kind=kOutput, calls=%fused_computation.6 | convolution fusion | flops 5804523520 | bytes 72155656 | tf_op jit(solution)/shard_map/qij,nj->qin/dot_general | solution.py:31
  139.9 0.1 reshape.68
  140.0 0.1 reduce_sum.19
  140.1 0.1 copy.12
  140.2 12.1 %all-reduce = f32[4,4,2]{0,2,1:T(2,128)S(1)} all-reduce(f32[4,4,2]{0,2,1:T(2,128)S(1)} %copy.12), channel_id=2, replica_groups=mesh['parts'=2,'cand'=4,'query'=4] {'cand'}, use_global_device_ids=true, to_apply=%region_2.3.clone | all-reduce | flops 32 | bytes 256
  152.3 1.1 constant_dynamic-slice_fusion.1
  (7 shorter events, 0.1 us)
Async XLA Ops:
  0.0 56.6 %copy-start = (bf16[4,8,13824]{2,1,0:T(8,128)(2,1)S(1)}, bf16[4,8,13824]{2,1,0:T(8,128)(2,1)}, u32[]{:S(2)}) copy-start(bf16[4,8,13824]{2,1,0:T(8,128)(2,1)} %param.10) | copy-start | bytes 2654212
  0.0 55.9 %copy-start.2 = (u32[32]{0:T(128)S(1)}, u32[32]{0:T(128)}, u32[]{:S(2)}) copy-start(u32[32]{0:T(128)} %constant.87) | copy-start | bytes 388
  0.0 56.6 %copy-start.1 = (bf16[4,8,5120]{2,1,0:T(8,128)(2,1)S(1)}, bf16[4,8,5120]{2,1,0:T(8,128)(2,1)}, u32[]{:S(2)}) copy-start(bf16[4,8,5120]{2,1,0:T(8,128)(2,1)} %param.9) | copy-start | bytes 983044
  4.2 12.8 %all-to-all-start.1 = ((bf16[4,2,4,2560]{3,2,1,0:T(4,128)(2,1)}), bf16[4,2,4,2560]{3,2,1,0:T(4,128)(2,1)S(1)}, u32[]{:S(2)}, u32[]{:S(2)}) async-start(bf16[4,2,4,2560]{3,2,1,0:T(4,128)(2,1)} %bitcast.7), calls=%async_computation.1 | async-start | bytes 327680 | tf_op jit(solution)/shard_map/all_to_all | solution.py:64
  17.9 38.6 %all-to-all-start = ((bf16[4,2,4,6912]{3,2,1,0:T(4,128)(2,1)}), bf16[4,2,4,6912]{3,2,1,0:T(4,128)(2,1)S(1)}, u32[]{:S(2)}, u32[]{:S(2)}) async-start(bf16[4,2,4,6912]{3,2,1,0:T(4,128)(2,1)} %bitcast.5), calls=%async_computation | async-start | bytes 884736 | tf_op jit(solution)/shard_map/all_to_all | solution.py:65
where the time goes:
time: 154 us; the launch traced here: 153 us
  matrix products  83.2 us (54%)
  other arithmetic  35.9 us (23%)
  blocking collectives  12.1 us (8%)
  starting transfers between devices  9.82 us (6%)
  local copies, waits for them, and re-layouts  8.04 us (5%)
  waiting for transfers between devices  4.23 us (3%)
    dot_general x1, matrix products, block_scores(): jnp.einsum('qij,nj->qin', precond, flat_in, preferred_element_type=jnp.fl...  83.2 us
    div x1, other arithmetic, body(): outer_sum / (eigenvalues[0].astype(jnp.float32) + DAMPING)  34.6 us
    unnamed x1, blocking collectives  12.1 us
    all_to_all x1, starting transfers between devices, body(): lax.all_to_all(out_parts, 'cand', split_axis=0, concat_axis=0, tiled=True)  6.36 us
    all_to_all x1, waiting for transfers between devices, body(): lax.all_to_all(out_parts, 'cand', split_axis=0, concat_axis=0, tiled=True)  4.23 us
    all_to_all x1, starting transfers between devices, body(): lax.all_to_all(in_parts, 'cand', split_axis=0, concat_axis=0, tiled=True)  3.46 us
  transfers between devices with their start and end apart: 2, of which 1 were waited for; matrix products, arithmetic and copies ran while one was open for 24% of the time, Pallas kernels for 0%

commit v1 on v0

v1 whole, which is shorter than its diff:
```python
import functools

import jax
import jax.numpy as jnp
from jax import lax
from jax.experimental import pallas as pl
from jax.experimental.pallas import tpu as pltpu
from jax.sharding import PartitionSpec as P

DAMPING = 0.05


def score_kernel(lam_ref, left_ref, right_ref, out_ref, acc_ref, *, width):
    @pl.when(pl.program_id(0) == 0)
    def _():
        acc_ref[...] = jnp.zeros_like(acc_ref)

    queries = left_ref.shape[0]

    @pl.loop(0, lam_ref.shape[1] // width)
    def _(chunk):
        if width == lam_ref.shape[1]:
            cols = slice(None)
        else:
            cols = pl.ds(pl.multiple_of(chunk * width, 128), width)
        inverse = 1.0 / (lam_ref[:, cols].astype(jnp.float32) + DAMPING)
        for q in range(queries):
            outer = jnp.dot(left_ref[q], right_ref[q, :, cols], preferred_element_type=jnp.float32)
            precond = (outer * inverse).astype(jnp.bfloat16)
            acc_ref[q, :, cols] += jnp.dot(
                out_ref[...], precond, preferred_element_type=jnp.float32
            )


def pick(total, unit, limit):
    best = total
    if total % unit == 0:
        for size in range(unit, min(total, limit) + 1, unit):
            if total % size == 0:
                best = size
    return best


def mapped_tokens(lam, left, right, out_tokens):
    rows, cols = lam.shape
    queries, depth = right.shape[:2]
    tokens = out_tokens.shape[0]
    height = pick(rows, 128, 256)
    width = pick(cols, 128, 2304)
    return pl.pallas_call(
        functools.partial(score_kernel, width=width),
        grid=(rows // height,),
        in_specs=[
            pl.BlockSpec((height, cols), lambda i: (i, 0)),
            pl.BlockSpec((queries, height, depth), lambda i: (0, i, 0)),
            pl.BlockSpec((queries, depth, cols), lambda i: (0, 0, 0)),
            pl.BlockSpec((tokens, height), lambda i: (0, i)),
        ],
        out_specs=pl.BlockSpec((queries, tokens, cols), lambda i: (0, 0, 0)),
        out_shape=jax.ShapeDtypeStruct((queries, tokens, cols), jnp.float32),
        compiler_params=pltpu.CompilerParams(vmem_limit_bytes=60 << 20),
        cost_estimate=pl.CostEstimate(
            flops=2 * queries * rows * cols * (depth + tokens),
            bytes_accessed=2 * rows * cols,
            transcendentals=rows * cols,
        ),
    )(lam, left, right, out_tokens)


def body(cand_out, cand_in, query_out, query_in, eigenvalues, slot_blocks, live_counts):
    tile_count = lax.axis_size("cand")
    row_tiles = min(8, max(2, tile_count // 8))
    col_tiles = tile_count // row_tiles
    position = lax.axis_index("cand")
    row_part = position // col_tiles
    col_part = position % col_tiles
    tokens = cand_out.shape[1]
    row_width = cand_out.shape[2] // row_tiles
    col_width = cand_in.shape[2] // col_tiles
    slot_count = slot_blocks.shape[2]
    queries = query_out.shape[0]

    own_slots = lax.dynamic_index_in_dim(slot_blocks[0], position, 0, keepdims=False)
    chosen_out = jnp.take(cand_out, own_slots, axis=0, mode="clip")
    chosen_in = jnp.take(cand_in, own_slots, axis=0, mode="clip")
    per_source = slot_count * tokens
    out_parts = jnp.moveaxis(chosen_out.reshape(per_source, row_tiles, row_width), 1, 0)
    out_parts = jnp.broadcast_to(
        out_parts[:, None], (row_tiles, col_tiles, per_source, row_width)
    ).reshape(tile_count, per_source, row_width)
    in_parts = jnp.moveaxis(chosen_in.reshape(per_source, col_tiles, col_width), 1, 0)
    in_parts = jnp.broadcast_to(
        in_parts[None], (row_tiles, col_tiles, per_source, col_width)
    ).reshape(tile_count, per_source, col_width)
    out_tokens = lax.all_to_all(out_parts, "cand", split_axis=0, concat_axis=0, tiled=True)
    in_tokens = lax.all_to_all(in_parts, "cand", split_axis=0, concat_axis=0, tiled=True)
    out_tokens = out_tokens.reshape(tile_count * per_source, row_width)
    in_tokens = in_tokens.reshape(tile_count * per_source, col_width)

    out_factor = lax.dynamic_slice_in_dim(query_out, row_part * row_width, row_width, 2)
    in_factor = lax.dynamic_slice_in_dim(query_in, col_part * col_width, col_width, 2)
    left = jnp.swapaxes(out_factor, 1, 2)

    mapped = mapped_tokens(eigenvalues[0], left, in_factor, out_tokens)
    totals = jnp.sum(mapped * in_tokens.astype(jnp.float32)[None], axis=2)
    totals = totals.reshape(queries, tile_count, slot_count, tokens).sum(axis=3)
    gathered = lax.all_to_all(
        jnp.moveaxis(totals, 1, 0), "cand", split_axis=0, concat_axis=0, tiled=True
    )
    scores = jnp.sum(gathered, axis=0)
    own_live = lax.dynamic_index_in_dim(live_counts[0], position, 0, keepdims=False)
    used = jnp.arange(slot_count, dtype=jnp.int32) < own_live
    return jnp.where(used[None], scores, 0.0)[:, None, :]


def solution(mesh):
    return jax.shard_map(
        body,
        mesh=mesh,
        in_specs=(
            P(("parts", "cand"), None, None),
            P(("parts", "cand"), None, None),
            P(("parts", "query"), None, None),
            P(("parts", "query"), None, None),
            P("cand", None, None),
            P(("parts", "query"), None, None),
            P(("parts", "query"), None),
        ),
        out_specs=P(("parts", "query"), "cand", None),
        check_vma=False,
    )
```

time: 154 us -> 105 us (0.68)
  matrix products: 83.2 us -> 0 us
  Pallas kernels: 0 us -> 66.6 us
  other arithmetic: 35.9 us -> 3.93 us
  blocking collectives: 12.1 us -> 0 us
  starting transfers between devices: 9.82 us -> 14.8 us
  waiting for transfers between devices: 4.23 us -> 8.67 us
  local copies, waits for them, and re-layouts: 8.04 us -> 10.1 us
    dot_general x1 -> x0, matrix products: 83.2 us -> none  [block_scores(): jnp.einsum('qij,nj->qin', precond, flat_in, preferred_element_type=jnp.fl...]
    pallas_call x0 -> x1, Pallas kernels: none -> 66.6 us  [mapped_tokens(): pl.pallas_call(functools.partial(score_kernel, width=width), grid=(rows /...]
    div x1 -> x0, other arithmetic: 34.6 us -> none  [body(): outer_sum / (eigenvalues[0].astype(jnp.float32) + DAMPING)]
    unnamed x1 -> x0, blocking collectives: 12.1 us -> none
    all_to_all x0 -> x1, starting transfers between devices: none -> 4.96 us  [body(): lax.all_to_all(jnp.moveaxis(totals, 1, 0), 'cand', split_axis=0, concat_a...]
    all_to_all x0 -> x1, waiting for transfers between devices: none -> 4.92 us  [body(): lax.all_to_all(jnp.moveaxis(totals, 1, 0), 'cand', split_axis=0, concat_a...]
    reduce_sum x1 -> x3, other arithmetic: 0.1 us -> 2.58 us  [the longest x1 2.46 us: body(): totals = jnp.sum(mapped * in_tokens.astype(jnp.float32)[None], axis=2)]
    gather x4 -> x2, local copies, waits for them, and re-layouts: 3.37 us -> 3.25 us  [the longest x1 1.72 us: body(): chosen_in = jnp.take(cand_in, own_slots, axis=0, mode='clip')]
  transfers between devices with their start and end apart: 2 -> 3, of which waited for: 1 -> 2; matrix products, arithmetic and copies ran while one was open for 24% -> 6% of each run, Pallas kernels for 0% -> 64%
where the time goes in v1:
time: 105 us; the launch traced here: 104 us
  Pallas kernels  66.6 us (63%)
  starting transfers between devices  14.8 us (14%)
  local copies, waits for them, and re-layouts  10.1 us (10%)
  waiting for transfers between devices  8.67 us (8%)
  other arithmetic  3.93 us (4%)
    pallas_call x1, Pallas kernels, mapped_tokens(): pl.pallas_call(functools.partial(score_kernel, width=width), grid=(rows /...  66.6 us
    all_to_all x1, starting transfers between devices, body(): lax.all_to_all(out_parts, 'cand', split_axis=0, concat_axis=0, tiled=True)  6.35 us
    all_to_all x1, starting transfers between devices, body(): lax.all_to_all(jnp.moveaxis(totals, 1, 0), 'cand', split_axis=0, concat_a...  4.96 us
    all_to_all x1, waiting for transfers between devices, body(): lax.all_to_all(jnp.moveaxis(totals, 1, 0), 'cand', split_axis=0, concat_a...  4.92 us
    all_to_all x1, waiting for transfers between devices, body(): lax.all_to_all(out_parts, 'cand', split_axis=0, concat_axis=0, tiled=True)  3.75 us
    all_to_all x1, starting transfers between devices, body(): lax.all_to_all(in_parts, 'cand', split_axis=0, concat_axis=0, tiled=True)  3.46 us
    reduce_sum x1, other arithmetic, body(): totals = jnp.sum(mapped * in_tokens.astype(jnp.float32)[None], axis=2)  2.46 us
  transfers between devices with their start and end apart: 3, of which 2 were waited for; matrix products, arithmetic and copies ran while one was open for 6% of the time, Pallas kernels for 64%

profile of v1, /device:TPU:0, one launch (start us, length us, event | category | flops | bytes accessed | tf_op | source)
XLA Modules:
  0.0 104.1 jit_solution(11440357551404868742)
XLA Ops:
  0.0 0.0 copy-start
  0.0 0.0 copy-start.2
  0.0 1.0 dynamic-slice_reduce_fusion
  1.0 1.5 %gather_fusion = bf16[2,4,5120]{2,1,0:T(4,128)(2,1)S(1)} fusion(bf16[3,4,5120]{2,1,0:T(4,128)(2,1)} %param.7, s32[1024]{0:T(1024)S(1)} %pad_clamp_fusion), kind=kCustom, calls=%fused_computation | custom fusion | bytes 163848 | tf_op jit(solution)/shard_map/jit(_take)/gather | solution.py:84
  2.6 0.7 broadcast_in_dim.35
  3.2 6.3 %all-to-all-start = ((bf16[4,8,2560]{2,1,0:T(8,128)(2,1)}), bf16[4,8,2560]{2,1,0:T(8,128)(2,1)S(1)}, u32[]{:S(2)}, u32[]{:S(2)}) async-start(bf16[4,8,2560]{2,1,0:T(8,128)(2,1)} %bitcast.4), calls=%async_computation | async-start | bytes 327680 | tf_op jit(solution)/shard_map/all_to_all | solution.py:95
  9.6 0.0 copy-start.3
  9.6 0.0 copy-done
  9.6 0.8 constant_dynamic-slice_fusion.right_ref
  10.4 1.7 %gather_fusion.1 = bf16[2,4,13824]{2,1,0:T(4,128)(2,1)S(1)} fusion(bf16[3,4,13824]{2,1,0:T(4,128)(2,1)} %param.8, s32[1024]{0:T(1024)S(1)} %pad_clamp_fusion), kind=kCustom, calls=%fused_computation.1 | custom fusion | bytes 442376 | tf_op jit(solution)/shard_map/jit(_take)/gather | solution.py:85
  12.1 0.1 reshape.65
  12.3 3.7 %all-to-all-done = bf16[4,8,2560]{2,1,0:T(8,128)(2,1)S(1)} async-done(((bf16[4,8,2560]{2,1,0:T(8,128)(2,1)}), bf16[4,8,2560]{2,1,0:T(8,128)(2,1)S(1)}, u32[]{:S(2)}, u32[]{:S(2)}) %all-to-all-start) | async-done | bytes 163872 | tf_op jit(solution)/shard_map/all_to_all | solution.py:95
  16.0 0.0 copy-start.1
  16.0 0.8 broadcast_in_dim.36
  16.8 3.5 %all-to-all-start.1 = ((bf16[4,8,6912]{2,1,0:T(8,128)(2,1)}), bf16[4,8,6912]{2,1,0:T(8,128)(2,1)S(1)}, u32[]{:S(2)}, u32[]{:S(2)}) async-start(bf16[4,8,6912]{2,1,0:T(8,128)(2,1)} %bitcast.7), calls=%async_computation.1 | async-start | bytes 884736 | tf_op jit(solution)/shard_map/all_to_all | solution.py:96
  20.3 0.0 copy-done.2
  20.3 2.0 %copy.18 = bf16[4,8,2560]{1,2,0:T(8,128)(2,1)} copy(bf16[4,8,2560]{2,1,0:T(8,128)(2,1)S(1)} %constant_dynamic-slice_fusion.1) | data formatting | bytes 327680
  22.3 0.0 copy-done.3
  22.3 0.6 constant_dynamic-slice_fusion.2
  22.9 0.0 copy-done.1
  22.9 66.6 %shard_map.73 = f32[4,32,6912]{2,1,0:T(8,128)} custom-call(bf16[2560,6912]{1,0:T(8,128)(2,1)} %bitcast.14, bf16[4,2560,8]{2,1,0:T(8,128)(2,1)} %bitcast.15, bf16[4,8,6912]{2,1,0:T(8,128)(2,1)} %constant_dynamic-slice_fusion.right_ref, bf16[32,2560]{1,0:T(8,128)(2,1)} %bitcast.17), custom_call_target="tpu_custom_call" | custom-call | flops 5662310400 | bytes 35389440 | tf_op jit(solution)/shard_map/pallas_call | solution.py:50
  89.5 0.0 all-to-all-done.1
  89.5 0.1 bitcast_convert_fusion
  89.6 2.5 %multiply_reduce_fusion = f32[4,32]{1,0:T(4,128)S(1)} fusion(f32[4,32,6912]{2,1,0:T(8,128)} %shard_map.73, f32[32,6912]{1,0:T(8,128)S(1)} %bitcast_convert_fusion), kind=kLoop, calls=%fused_computation.2 | loop fusion | flops 1769344 | bytes 4424192 | tf_op jit(solution)/shard_map/reduce_sum | solution.py:105
  92.0 0.1 reshape.67
  92.1 0.1 reduce_sum.30
  92.2 0.7 copy.17
  92.9 5.0 %all-to-all-start.2 = ((f32[4,4,2]{1,2,0:T(2,128)}), f32[4,4,2]{1,2,0:T(2,128)S(1)}, u32[]{:S(2)}, u32[]{:S(2)}) async-start(f32[4,4,2]{1,2,0:T(2,128)} %copy.17), calls=%async_computation.2 | async-start | bytes 8192 | tf_op jit(solution)/shard_map/all_to_all | solution.py:107
  97.9 0.6 iota_compare_fusion
  98.5 4.9 %all-to-all-done.2 = f32[4,4,2]{1,2,0:T(2,128)S(1)} async-done(((f32[4,4,2]{1,2,0:T(2,128)}), f32[4,4,2]{1,2,0:T(2,128)S(1)}, u32[]{:S(2)}, u32[]{:S(2)}) %all-to-all-start.2) | async-done | bytes 160 | tf_op jit(solution)/shard_map/all_to_all | solution.py:107
  103.5 0.6 bitcast_select_fusion
  (6 shorter events, 0.1 us)
Async XLA Ops:
  0.0 9.6 %copy-start = (bf16[4,8,13824]{2,1,0:T(8,128)(2,1)S(1)}, bf16[4,8,13824]{2,1,0:T(8,128)(2,1)}, u32[]{:S(2)}) copy-start(bf16[4,8,13824]{2,1,0:T(8,128)(2,1)} %param.10) | copy-start | bytes 2654212
  0.0 20.3 %copy-start.2 = (bf16[4,8,5120]{2,1,0:T(8,128)(2,1)S(1)}, bf16[4,8,5120]{2,1,0:T(8,128)(2,1)}, u32[]{:S(2)}) copy-start(bf16[4,8,5120]{2,1,0:T(8,128)(2,1)} %param.9) | copy-start | bytes 983044
  3.2 12.8 %all-to-all-start = ((bf16[4,8,2560]{2,1,0:T(8,128)(2,1)}), bf16[4,8,2560]{2,1,0:T(8,128)(2,1)S(1)}, u32[]{:S(2)}, u32[]{:S(2)}) async-start(bf16[4,8,2560]{2,1,0:T(8,128)(2,1)} %bitcast.4), calls=%async_computation | async-start | bytes 327680 | tf_op jit(solution)/shard_map/all_to_all | solution.py:95
  9.6 12.7 %copy-start.3 = (s32[1,4]{1,0:T(1,128)S(1)}, s32[1,4]{1,0:T(1,128)}, u32[]{:S(2)}) copy-start(s32[1,4]{1,0:T(1,128)} %param.13) | copy-start | bytes 52
  16.0 6.9 %copy-start.1 = (bf16[4,8,2560]{2,1,0:T(8,128)(2,1)}, bf16[4,8,2560]{2,1,0:T(8,128)(2,1)S(1)}, u32[]{:S(2)}) copy-start(bf16[4,8,2560]{2,1,0:T(8,128)(2,1)S(1)} %all-to-all-done) | copy-start | bytes 491524
  16.8 72.7 %all-to-all-start.1 = ((bf16[4,8,6912]{2,1,0:T(8,128)(2,1)}), bf16[4,8,6912]{2,1,0:T(8,128)(2,1)S(1)}, u32[]{:S(2)}, u32[]{:S(2)}) async-start(bf16[4,8,6912]{2,1,0:T(8,128)(2,1)} %bitcast.7), calls=%async_computation.1 | async-start | bytes 884736 | tf_op jit(solution)/shard_map/all_to_all | solution.py:96
  92.9 10.5 %all-to-all-start.2 = ((f32[4,4,2]{1,2,0:T(2,128)}), f32[4,4,2]{1,2,0:T(2,128)S(1)}, u32[]{:S(2)}, u32[]{:S(2)}) async-start(f32[4,4,2]{1,2,0:T(2,128)} %copy.17), calls=%async_computation.2 | async-start | bytes 8192 | tf_op jit(solution)/shard_map/all_to_all | solution.py:107

commit v2 on v1

v2 whole, which is shorter than its diff:
```python
import functools

import jax
import jax.numpy as jnp
from jax import lax
from jax.experimental import pallas as pl
from jax.experimental.pallas import tpu as pltpu
from jax.sharding import PartitionSpec as P

DAMPING = 0.05
PIECE = 512
BEHIND = 2
MAX_SHIFTS = 8


def pack_kernel(place_ref, *refs, slots, shifts, row_tiles, col_tiles, by_shift):
    outs, ins = refs[:slots], refs[slots : 2 * slots]
    results = refs[2 * slots :]
    position = place_ref[slots]
    tokens = outs[0].shape[1]
    row_width = outs[0].shape[2] // row_tiles
    col_width = ins[0].shape[2] // col_tiles

    def store(sources, target, part, width, parts):
        for piece in range(parts):

            @pl.when(part == piece)
            def _():
                for slot, source in enumerate(sources):
                    target[slot * tokens : (slot + 1) * tokens, :] = source[
                        0, :, piece * width : (piece + 1) * width
                    ]

    for shift in range(shifts):
        if by_shift:
            tile = lax.rem(position + shift, shifts)
            targets = results[shift], results[shifts + shift]
        else:
            tile = jnp.int32(shift)
            targets = results[0].at[shift], results[1].at[shift]
        store(outs, targets[0], tile // col_tiles, row_width, row_tiles)
        store(ins, targets[1], lax.rem(tile, col_tiles), col_width, col_tiles)


def pack_tokens(cand_out, cand_in, own_slots, position, row_tiles, col_tiles, shifts, by_shift):
    slots = own_slots.shape[0]
    tokens = cand_out.shape[1]
    rows = slots * tokens
    widths = cand_out.shape[2] // row_tiles, cand_in.shape[2] // col_tiles
    place = jnp.concatenate([own_slots, position[None].astype(jnp.int32)])

    def listed(slot):
        return lambda i, place_ref: (place_ref[slot], 0, 0)

    specs = [
        pl.BlockSpec((1, tokens, array.shape[2]), listed(slot))
        for array in (cand_out, cand_in)
        for slot in range(slots)
    ]
    if by_shift:
        shapes = [(rows, width) for width in widths for _ in range(shifts)]
    else:
        shapes = [(shifts, rows, width) for width in widths]
    return pl.pallas_call(
        functools.partial(
            pack_kernel,
            slots=slots,
            shifts=shifts,
            row_tiles=row_tiles,
            col_tiles=col_tiles,
            by_shift=by_shift,
        ),
        grid_spec=pltpu.PrefetchScalarGridSpec(
            num_scalar_prefetch=1,
            grid=(1,),
            in_specs=specs,
            out_specs=[
                pl.BlockSpec(shape, lambda i, place_ref, n=len(shape): (0,) * n)
                for shape in shapes
            ],
        ),
        out_shape=[jax.ShapeDtypeStruct(shape, cand_out.dtype) for shape in shapes],
    )(place, *([cand_out] * slots), *([cand_in] * slots))


def map_kernel(part_ref, lam_ref, left_ref, right_ref, *refs):
    del part_ref
    out_refs, acc_ref, out_buf = refs[:-2], refs[-2], refs[-1]

    @pl.when(pl.program_id(0) == 0)
    def _():
        acc_ref[...] = jnp.zeros_like(acc_ref)

    start = 0
    for ref in out_refs:
        out_buf[start : start + ref.shape[0], :] = ref[...]
        start += ref.shape[0]
    queries = left_ref.shape[0]
    cols = lam_ref.shape[2]
    lefts = [left_ref[q].astype(jnp.float32).T.astype(jnp.bfloat16) for q in range(queries)]
    waiting = []

    def contract():
        q, begin, end, precond = waiting.pop(0)
        acc_ref[q, :, begin:end] += jnp.dot(
            out_buf[...], precond, preferred_element_type=jnp.float32
        )

    for begin in range(0, cols, PIECE):
        end = min(begin + PIECE, cols)
        inverse = 1.0 / (lam_ref[0, :, begin:end].astype(jnp.float32) + DAMPING)
        for q in range(queries):
            outer = jnp.dot(
                lefts[q], right_ref[q, :, begin:end], preferred_element_type=jnp.float32
            )
            if len(waiting) >= BEHIND:
                contract()
            waiting.append((q, begin, end, (outer * inverse).astype(jnp.bfloat16)))
    while waiting:
        contract()


def pick(total, unit, limit):
    best = total
    if total % unit == 0:
        for size in range(unit, min(total, limit) + 1, unit):
            if total % size == 0:
                best = size
    return best


def map_tokens(lam, query_out, query_in, row_part, col_part, out_tokens):
    rows, cols = lam.shape[1:]
    queries, depth = query_in.shape[:2]
    tokens = sum(part.shape[0] for part in out_tokens)
    height = pick(rows, 128, 256)
    steps = rows // height
    if cols % 128:
        query_in = lax.dynamic_slice_in_dim(query_in, col_part * cols, cols, 2)
        col_part = jnp.zeros_like(col_part)
    parts = jnp.stack([row_part, col_part]).astype(jnp.int32)
    grant = (16 << 20) + 8 * queries * tokens * cols + 4 * height * cols
    return pl.pallas_call(
        map_kernel,
        grid_spec=pltpu.PrefetchScalarGridSpec(
            num_scalar_prefetch=1,
            grid=(steps,),
            in_specs=[
                pl.BlockSpec((1, height, cols), lambda i, part: (0, i, 0)),
                pl.BlockSpec((queries, depth, height), lambda i, part: (0, 0, part[0] * steps + i)),
                pl.BlockSpec((queries, depth, cols), lambda i, part: (0, 0, part[1])),
            ]
            + [pl.BlockSpec((part.shape[0], height), lambda i, part: (0, i)) for part in out_tokens],
            out_specs=pl.BlockSpec((queries, tokens, cols), lambda i, part: (0, 0, 0)),
            scratch_shapes=[pltpu.VMEM((tokens, height), jnp.bfloat16)],
        ),
        out_shape=jax.ShapeDtypeStruct((queries, tokens, cols), jnp.float32),
        compiler_params=pltpu.CompilerParams(vmem_limit_bytes=grant),
        cost_estimate=pl.CostEstimate(
            flops=2 * queries * rows * cols * (depth + tokens),
            bytes_accessed=2 * rows * cols,
            transcendentals=rows * cols,
        ),
    )(parts, lam, query_out, query_in, *out_tokens)


def fold_kernel(mapped_ref, *refs):
    half = len(refs) // 2
    start = 0
    for in_ref, score_ref in zip(refs[:half], refs[half:]):
        stop = start + in_ref.shape[0]
        product = mapped_ref[:, start:stop, :] * in_ref[...].astype(jnp.float32)[None]
        part = jnp.sum(product, axis=2)
        start = stop

        @pl.when(pl.program_id(0) == 0)
        def _():
            score_ref[...] = part

        @pl.when(pl.program_id(0) > 0)
        def _():
            score_ref[...] += part


def fold_tokens(mapped, in_tokens):
    queries, tokens, cols = mapped.shape
    width = pick(cols, 128, 1536)
    grant = min((4 << 20) + 24 * queries * tokens * width, 56 << 20)
    return pl.pallas_call(
        fold_kernel,
        grid=(cols // width,),
        in_specs=[pl.BlockSpec((queries, tokens, width), lambda i: (0, 0, i))]
        + [pl.BlockSpec((part.shape[0], width), lambda i: (0, i)) for part in in_tokens],
        out_specs=[pl.BlockSpec((queries, part.shape[0]), lambda i: (0, 0)) for part in in_tokens],
        out_shape=[
            jax.ShapeDtypeStruct((queries, part.shape[0]), jnp.float32) for part in in_tokens
        ],
        compiler_params=pltpu.CompilerParams(vmem_limit_bytes=grant),
    )(mapped, *in_tokens)


def exchange(array):
    return lax.all_to_all(array, "cand", split_axis=0, concat_axis=0, tiled=True)


def shifted(array, shift, devices):
    pairs = [(device, (device + shift) % devices) for device in range(devices)]
    return lax.ppermute(array, "cand", pairs)


def body(cand_out, cand_in, query_out, query_in, eigenvalues, slot_blocks, live_counts):
    tile_count = lax.axis_size("cand")
    row_tiles = min(8, max(2, tile_count // 8))
    col_tiles = tile_count // row_tiles
    position = lax.axis_index("cand")
    row_part = position // col_tiles
    col_part = position % col_tiles
    tokens = cand_out.shape[1]
    slot_count = slot_blocks.shape[2]
    queries = query_out.shape[0]
    by_shift = tile_count <= MAX_SHIFTS

    own_slots = lax.dynamic_index_in_dim(slot_blocks[0], position, 0, keepdims=False)
    packed = pack_tokens(
        cand_out, cand_in, own_slots, position, row_tiles, col_tiles, tile_count, by_shift
    )
    if by_shift:
        out_tokens = [packed[0]] + [
            shifted(packed[shift], shift, tile_count) for shift in range(1, tile_count)
        ]
        in_tokens = [packed[tile_count]] + [
            shifted(packed[tile_count + shift], shift, tile_count)
            for shift in range(1, tile_count)
        ]
    else:
        out_tokens = [exchange(packed[0]).reshape(-1, packed[0].shape[2])]
        in_tokens = [exchange(packed[1]).reshape(-1, packed[1].shape[2])]

    mapped = map_tokens(eigenvalues, query_out, query_in, row_part, col_part, out_tokens)
    folded = fold_tokens(mapped, in_tokens)
    if by_shift:
        total = folded[0]
        for shift in range(1, tile_count):
            total = total + shifted(folded[shift], -shift, tile_count)
    else:
        parts = jnp.moveaxis(folded[0].reshape(queries, tile_count, -1), 1, 0)
        total = jnp.sum(exchange(parts), axis=0)
    scores = total.reshape(queries, slot_count, tokens).sum(axis=2)
    own_live = lax.dynamic_index_in_dim(live_counts[0], position, 0, keepdims=False)
    used = jnp.arange(slot_count, dtype=jnp.int32) < own_live
    return jnp.where(used[None], scores, 0.0)[:, None, :]


def solution(mesh):
    return jax.shard_map(
        body,
        mesh=mesh,
        in_specs=(
            P(("parts", "cand"), None, None),
            P(("parts", "cand"), None, None),
            P(("parts", "query"), None, None),
            P(("parts", "query"), None, None),
            P("cand", None, None),
            P(("parts", "query"), None, None),
            P(("parts", "query"), None),
        ),
        out_specs=P(("parts", "query"), "cand", None),
        check_vma=False,
    )
```

time: 105 us -> 81.1 us (0.77)
  Pallas kernels: 66.6 us -> 55.1 us
  waiting for transfers between devices: 8.67 us -> 3.45 us
  local copies, waits for them, and re-layouts: 10.1 us -> 5.2 us
  other arithmetic: 3.93 us -> 2.11 us
    ppermute x0 -> x9, starting transfers between devices: none -> 14.9 us  [shifted(): return lax.ppermute(array, 'cand', pairs)]
    all_to_all x3 -> x0, starting transfers between devices: 14.8 us -> none  [the longest x1 6.35 us: body(): lax.all_to_all(out_parts, 'cand', split_axis=0, concat_axis=0, tiled=True)]
    pallas_call x1 -> x3, Pallas kernels: 66.6 us -> 55.1 us  [the longest x1 49.8 us: map_tokens(): pl.pallas_call(map_kernel, grid_spec=pltpu.PrefetchScalarGridSpec(num_sca...]
    all_to_all x3 -> x0, waiting for transfers between devices: 8.67 us -> none  [the longest x1 4.92 us: body(): lax.all_to_all(jnp.moveaxis(totals, 1, 0), 'cand', split_axis=0, concat_a...]
    ppermute x0 -> x9, waiting for transfers between devices: none -> 3.45 us  [shifted(): return lax.ppermute(array, 'cand', pairs)]
    gather x2 -> x0, local copies, waits for them, and re-layouts: 3.25 us -> none  [the longest x1 1.72 us: body(): chosen_in = jnp.take(cand_in, own_slots, axis=0, mode='clip')]
    reduce_sum x3 -> x1, other arithmetic: 2.58 us -> 0.09 us  [body(): scores = total.reshape(queries, slot_count, tokens).sum(axis=2)]
    unnamed x9 -> x10, local copies, waits for them, and re-layouts: 2 us -> 3.6 us
  transfers between devices with their start and end apart: 3 -> 9, of which waited for: 2 -> 2; matrix products, arithmetic and copies ran while one was open for 6% -> 2% of each run, Pallas kernels for 64% -> 62%
where the time goes in v2:
time: 81.1 us; the launch traced here: 80.8 us
  Pallas kernels  55.1 us (68%)
  starting transfers between devices  14.9 us (18%)
  local copies, waits for them, and re-layouts  5.2 us (6%)
  waiting for transfers between devices  3.45 us (4%)
  other arithmetic  2.11 us (3%)
    pallas_call x1, Pallas kernels, map_tokens(): pl.pallas_call(map_kernel, grid_spec=pltpu.PrefetchScalarGridSpec(num_sca...  49.8 us
    ppermute x9, starting transfers between devices, shifted(): return lax.ppermute(array, 'cand', pairs)  14.9 us
    unnamed x10, local copies, waits for them, and re-layouts  3.6 us
    ppermute x9, waiting for transfers between devices, shifted(): return lax.ppermute(array, 'cand', pairs)  3.45 us
    pallas_call x1, Pallas kernels, pack_tokens(): pl.pallas_call(functools.partial(pack_kernel, slots=slots, shifts=shifts,...  2.71 us
    pallas_call x1, Pallas kernels, fold_tokens(): pl.pallas_call(fold_kernel, grid=(cols // width,), in_specs=[pl.BlockSpec...  2.6 us
  transfers between devices with their start and end apart: 9, of which 2 were waited for; matrix products, arithmetic and copies ran while one was open for 2% of the time, Pallas kernels for 62%

profile of v2, /device:TPU:0, one launch (start us, length us, event | category | flops | bytes accessed | tf_op | source)
XLA Modules:
  0.0 80.8 jit_solution(14332153077701241589)
XLA Ops:
  0.0 0.7 copy-done
  0.7 0.2 dynamic-slice_reduce_fusion
  0.9 0.7 pad_add_fusion.1.place_ref
  1.5 2.7 %shard_map.73 = (bf16[8,2560]{1,0:T(8,128)(2,1)}, bf16[8,2560]{1,0:T(8,128)(2,1)}, bf16[8,2560]{1,0:T(8,128)(2,1)}, bf16[8,2560]{1,0:T(8,128)(2,1)}, bf16[8,6912...) custom-call(s32[3]{0:T(128)} %pad_add_fusion.1.place_ref, ...), custom_call_target="tpu_custom_call" | custom-call | tf_op jit(solution)/shard_map/pallas_call | solution.py:64
  4.2 3.1 %collective-permute-start = (bf16[8,2560]{1,0:T(8,128)(2,1)}, bf16[8,2560]{1,0:T(8,128)(2,1)S(1)}, u32[]{:S(2)}, u32[]{:S(2)}) collective-permute-start(bf16[8,2560]{1,0:T(8,128)(2,1)} %get-tuple-element.18), channel_id=1, source_target_pairs={{0,4},{4,8},{8,12},{12,0},{1,5},{5,9},{9,13},{13,1},{2,6},{6,10},{... | collective-permute-start | bytes 122888 | tf_op jit(solution)/shard_map/ppermute | solution.py:208
  7.3 2.6 %collective-permute-start.1 = (bf16[8,2560]{1,0:T(8,128)(2,1)}, bf16[8,2560]{1,0:T(8,128)(2,1)S(1)}, u32[]{:S(2)}, u32[]{:S(2)}) collective-permute-start(bf16[8,2560]{1,0:T(8,128)(2,1)} %get-tuple-element.19), channel_id=1, source_target_pairs={{0,8},{4,12},{8,0},{12,4},{1,9},{5,13},{9,1},{13,5},{2,10},{6,14},... | collective-permute-start | bytes 122888 | tf_op jit(solution)/shard_map/ppermute | solution.py:208
  9.9 1.3 %collective-permute-start.2 = (bf16[8,2560]{1,0:T(8,128)(2,1)}, bf16[8,2560]{1,0:T(8,128)(2,1)S(1)}, u32[]{:S(2)}, u32[]{:S(2)}) collective-permute-start(bf16[8,2560]{1,0:T(8,128)(2,1)} %get-tuple-element.20), channel_id=1, source_target_pairs={{0,12},{4,0},{8,4},{12,8},{1,13},{5,1},{9,5},{13,9},{2,14},{6,2},{... | collective-permute-start | bytes 122888 | tf_op jit(solution)/shard_map/ppermute | solution.py:208
  11.2 0.7 collective-permute-start.3
  11.9 0.3 collective-permute-start.4
  12.2 1.2 %constant_dynamic-slice_fusion = s32[1,1]{1,0:T(1,128)} fusion(s32[1,4]{1,0:T(1,128)} %param.13, s32[]{:T(128)S(6)} %select_n.28), kind=kLoop, calls=%fused_computation.5 | loop fusion | bytes 12 | tf_op jit(solution)/shard_map/jit(dynamic_index_in_dim)/dynamic_slice | solution.py:249
  13.5 0.6 iota_compare_fusion
  14.1 0.1 pad_add_fusion.part_ref
  14.2 0.0 collective-permute-done.refs_1_
  14.2 2.8 %collective-permute-start.5 = (bf16[8,6912]{1,0:T(8,128)(2,1)}, bf16[8,6912]{1,0:T(8,128)(2,1)S(1)}, u32[]{:S(2)}, u32[]{:S(2)}) collective-permute-start(bf16[8,6912]{1,0:T(8,128)(2,1)} %get-tuple-element.24), channel_id=1, source_target_pairs={{0,12},{4,0},{8,4},{12,8},{1,13},{5,1},{9,5},{13,9},{2,14},{6,2},{... | collective-permute-start | bytes 331784 | tf_op jit(solution)/shard_map/ppermute | solution.py:208
  17.0 0.0 collective-permute-done.1.refs_2_
  17.0 1.2 %copy-done.1 = bf16[4,8,13824]{2,1,0:T(8,128)(2,1)S(1)} copy-done((bf16[4,8,13824]{2,1,0:T(8,128)(2,1)S(1)}, bf16[4,8,13824]{2,1,0:T(8,128)(2,1)}, u32[]{:S(2)}) %copy-start.1) | copy-done | bytes 884760
  18.2 1.0 %copy-done.2 = bf16[4,8,5120]{2,1,0:T(8,128)(2,1)S(1)} copy-done((bf16[4,8,5120]{2,1,0:T(8,128)(2,1)S(1)}, bf16[4,8,5120]{2,1,0:T(8,128)(2,1)}, u32[]{:S(2)}) %copy-start.2) | copy-done | bytes 327704
  19.2 0.8 copy-done.4
  20.0 49.8 %shard_map.74.mapped_ref = f32[4,32,6912]{2,1,0:T(8,128)S(1)} custom-call(s32[2]{0:T(128)S(1)} %pad_add_fusion.part_ref, bf16[1,2560,6912]{2,1,0:T(8,128)(2,1)} %lam_ref.1, bf16[4,8,5120]{2,1,0:T(8,128)(2,1)S(1)} %copy-done.2, bf16[4,8,13824]{2,1,0:T(8,128)(2,1)S(1)} %copy-done.1, bf16[8,2560]{1,0:T(8,128)(2,1)S(1)} %copy-done.4, ...), custom_call_target="tpu_custom_call" | custom-call | flops 5662310400 | bytes 35389440 | tf_op jit(solution)/shard_map/pallas_call | solution.py:143
  69.7 0.0 collective-permute-done.3.refs_1_
  69.7 0.0 collective-permute-done.5.refs_3_
  69.8 2.6 %shard_map.75 = (f32[4,8]{1,0:T(4,128)S(1)}, f32[4,8]{1,0:T(4,128)S(1)}, f32[4,8]{1,0:T(4,128)S(1)}, f32[4,8]{1,0:T(4,128)S(1)}) custom-call(f32[4,32,6912]{2,1,0:T(8,128)S(1)} %shard_map.74.mapped_ref, bf16[8,6912]{1,0:T(8,128)(2,1)S(1)} %copy-done.3, bf16[8,6912]{1,0:T(8,128)(2,1)S(1)} %collective-permute-done.3.refs_1_, ...), custom_call_target="tpu_custom_call" | custom-call | tf_op jit(solution)/shard_map/pallas_call | solution.py:189
  72.4 1.3 %collective-permute-start.6 = (f32[4,8]{1,0:T(4,128)S(1)}, f32[4,8]{1,0:T(4,128)S(1)}, u32[]{:S(2)}, u32[]{:S(2)}) collective-permute-start(f32[4,8]{1,0:T(4,128)S(1)} %get-tuple-element.26), channel_id=1, source_target_pairs={{0,12},{4,0},{8,4},{12,8},{1,13},{5,1},{9,5},{13,9},{2,14},{6,2},{... | collective-permute-start | bytes 392 | tf_op jit(solution)/shard_map/ppermute | solution.py:208
  73.6 0.9 %collective-permute-start.7 = (f32[4,8]{1,0:T(4,128)S(1)}, f32[4,8]{1,0:T(4,128)S(1)}, u32[]{:S(2)}, u32[]{:S(2)}) collective-permute-start(f32[4,8]{1,0:T(4,128)S(1)} %get-tuple-element.27), channel_id=1, source_target_pairs={{0,8},{4,12},{8,0},{12,4},{1,9},{5,13},{9,1},{13,5},{2,10},{6,14},... | collective-permute-start | bytes 392 | tf_op jit(solution)/shard_map/ppermute | solution.py:208
  74.5 1.9 %collective-permute-start.8 = (f32[4,8]{1,0:T(4,128)S(1)}, f32[4,8]{1,0:T(4,128)S(1)}, u32[]{:S(2)}, u32[]{:S(2)}) collective-permute-start(f32[4,8]{1,0:T(4,128)S(1)} %get-tuple-element.28), channel_id=1, source_target_pairs={{0,4},{4,8},{8,12},{12,0},{1,5},{5,9},{9,13},{13,1},{2,6},{6,10},{... | collective-permute-start | bytes 392 | tf_op jit(solution)/shard_map/ppermute | solution.py:208
  76.4 0.0 collective-permute-done.6
  76.4 1.7 %collective-permute-done.7 = f32[4,8]{1,0:T(4,128)S(1)} collective-permute-done((f32[4,8]{1,0:T(4,128)S(1)}, f32[4,8]{1,0:T(4,128)S(1)}, u32[]{:S(2)}, u32[]{:S(2)}) %collective-permute-start.7) | collective-permute-done | bytes 160 | tf_op jit(solution)/shard_map/ppermute | solution.py:208
  78.1 1.8 %collective-permute-done.8 = f32[4,8]{1,0:T(4,128)S(1)} collective-permute-done((f32[4,8]{1,0:T(4,128)S(1)}, f32[4,8]{1,0:T(4,128)S(1)}, u32[]{:S(2)}, u32[]{:S(2)}) %collective-permute-start.8) | collective-permute-done | bytes 160 | tf_op jit(solution)/shard_map/ppermute | solution.py:208
  79.9 0.1 reshape.36
  80.0 0.1 reduce_sum.11
  80.1 0.1 copy.8
  80.1 0.6 bitcast_select_fusion
  (9 shorter events, 0.0 us)
Async XLA Ops:
  0.0 0.7 copy-start
  4.2 10.0 %collective-permute-start = (bf16[8,2560]{1,0:T(8,128)(2,1)}, bf16[8,2560]{1,0:T(8,128)(2,1)S(1)}, u32[]{:S(2)}, u32[]{:S(2)}) collective-permute-start(bf16[8,2560]{1,0:T(8,128)(2,1)} %get-tuple-element.18), channel_id=1, source_target_pairs={{0,4},{4,8},{8,12},{12,0},{1,5},{5,9},{9,13},{13,1},{2,6},{6,10},{... | collective-permute-start | bytes 122888 | tf_op jit(solution)/shard_map/ppermute | solution.py:208
  7.3 9.8 %collective-permute-start.1 = (bf16[8,2560]{1,0:T(8,128)(2,1)}, bf16[8,2560]{1,0:T(8,128)(2,1)S(1)}, u32[]{:S(2)}, u32[]{:S(2)}) collective-permute-start(bf16[8,2560]{1,0:T(8,128)(2,1)} %get-tuple-element.19), channel_id=1, source_target_pairs={{0,8},{4,12},{8,0},{12,4},{1,9},{5,13},{9,1},{13,5},{2,10},{6,14},... | collective-permute-start | bytes 122888 | tf_op jit(solution)/shard_map/ppermute | solution.py:208
  9.9 7.2 %collective-permute-start.2 = (bf16[8,2560]{1,0:T(8,128)(2,1)}, bf16[8,2560]{1,0:T(8,128)(2,1)S(1)}, u32[]{:S(2)}, u32[]{:S(2)}) collective-permute-start(bf16[8,2560]{1,0:T(8,128)(2,1)} %get-tuple-element.20), channel_id=1, source_target_pairs={{0,12},{4,0},{8,4},{12,8},{1,13},{5,1},{9,5},{13,9},{2,14},{6,2},{... | collective-permute-start | bytes 122888 | tf_op jit(solution)/shard_map/ppermute | solution.py:208
  11.2 58.5 %collective-permute-start.3 = (bf16[8,6912]{1,0:T(8,128)(2,1)}, bf16[8,6912]{1,0:T(8,128)(2,1)S(1)}, u32[]{:S(2)}, u32[]{:S(2)}) collective-permute-start(bf16[8,6912]{1,0:T(8,128)(2,1)} %get-tuple-element.22), channel_id=1, source_target_pairs={{0,4},{4,8},{8,12},{12,0},{1,5},{5,9},{9,13},{13,1},{2,6},{6,10},{... | collective-permute-start | bytes 331784 | tf_op jit(solution)/shard_map/ppermute | solution.py:208
  11.9 57.9 %collective-permute-start.4 = (bf16[8,6912]{1,0:T(8,128)(2,1)}, bf16[8,6912]{1,0:T(8,128)(2,1)S(1)}, u32[]{:S(2)}, u32[]{:S(2)}) collective-permute-start(bf16[8,6912]{1,0:T(8,128)(2,1)} %get-tuple-element.23), channel_id=1, source_target_pairs={{0,8},{4,12},{8,0},{12,4},{1,9},{5,13},{9,1},{13,5},{2,10},{6,14},... | collective-permute-start | bytes 331784 | tf_op jit(solution)/shard_map/ppermute | solution.py:208
  14.2 55.5 %collective-permute-start.5 = (bf16[8,6912]{1,0:T(8,128)(2,1)}, bf16[8,6912]{1,0:T(8,128)(2,1)S(1)}, u32[]{:S(2)}, u32[]{:S(2)}) collective-permute-start(bf16[8,6912]{1,0:T(8,128)(2,1)} %get-tuple-element.24), channel_id=1, source_target_pairs={{0,12},{4,0},{8,4},{12,8},{1,13},{5,1},{9,5},{13,9},{2,14},{6,2},{... | collective-permute-start | bytes 331784 | tf_op jit(solution)/shard_map/ppermute | solution.py:208
  17.0 1.2 %copy-start.1 = (bf16[4,8,13824]{2,1,0:T(8,128)(2,1)S(1)}, bf16[4,8,13824]{2,1,0:T(8,128)(2,1)}, u32[]{:S(2)}) copy-start(bf16[4,8,13824]{2,1,0:T(8,128)(2,1)} %right_ref.1) | copy-start | bytes 2654212
  18.2 1.0 %copy-start.2 = (bf16[4,8,5120]{2,1,0:T(8,128)(2,1)S(1)}, bf16[4,8,5120]{2,1,0:T(8,128)(2,1)}, u32[]{:S(2)}) copy-start(bf16[4,8,5120]{2,1,0:T(8,128)(2,1)} %left_ref.1) | copy-start | bytes 983044
  19.2 0.8 copy-start.4
  20.0 49.8 %copy-start.3 = (bf16[8,6912]{1,0:T(8,128)(2,1)S(1)}, bf16[8,6912]{1,0:T(8,128)(2,1)}, u32[]{:S(2)}) copy-start(bf16[8,6912]{1,0:T(8,128)(2,1)} %get-tuple-element.21.refs_0_) | copy-start | bytes 331780
  72.4 4.1 %collective-permute-start.6 = (f32[4,8]{1,0:T(4,128)S(1)}, f32[4,8]{1,0:T(4,128)S(1)}, u32[]{:S(2)}, u32[]{:S(2)}) collective-permute-start(f32[4,8]{1,0:T(4,128)S(1)} %get-tuple-element.26), channel_id=1, source_target_pairs={{0,12},{4,0},{8,4},{12,8},{1,13},{5,1},{9,5},{13,9},{2,14},{6,2},{... | collective-permute-start | bytes 392 | tf_op jit(solution)/shard_map/ppermute | solution.py:208
  73.6 4.5 %collective-permute-start.7 = (f32[4,8]{1,0:T(4,128)S(1)}, f32[4,8]{1,0:T(4,128)S(1)}, u32[]{:S(2)}, u32[]{:S(2)}) collective-permute-start(f32[4,8]{1,0:T(4,128)S(1)} %get-tuple-element.27), channel_id=1, source_target_pairs={{0,8},{4,12},{8,0},{12,4},{1,9},{5,13},{9,1},{13,5},{2,10},{6,14},... | collective-permute-start | bytes 392 | tf_op jit(solution)/shard_map/ppermute | solution.py:208
  74.5 5.4 %collective-permute-start.8 = (f32[4,8]{1,0:T(4,128)S(1)}, f32[4,8]{1,0:T(4,128)S(1)}, u32[]{:S(2)}, u32[]{:S(2)}) collective-permute-start(f32[4,8]{1,0:T(4,128)S(1)} %get-tuple-element.28), channel_id=1, source_target_pairs={{0,4},{4,8},{8,12},{12,0},{1,5},{5,9},{9,13},{13,1},{2,6},{6,10},{... | collective-permute-start | bytes 392 | tf_op jit(solution)/shard_map/ppermute | solution.py:208

commit v3 on v1

v3 whole, which is shorter than its diff:
```python
import functools

import jax
import jax.numpy as jnp
from jax import lax
from jax.experimental import pallas as pl
from jax.experimental.pallas import tpu as pltpu
from jax.sharding import PartitionSpec as P

DAMPING = 0.05
PIECE = 512
BEHIND = 2
MAX_SHIFTS = 8
GRANT_AHEAD = 62 << 20
GRANT_MAIN = 48 << 20
GRANT_AHEAD = 48 << 20
GRANT_MAIN = 48 << 20


def pack_kernel(list_ref, out_ref, in_ref, *results, row_tiles, col_tiles, shifts, by_shift):
    position = lax.axis_index("cand")
    slots = list_ref.shape[1]
    tokens = out_ref.shape[1]
    row_width = out_ref.shape[2] // row_tiles
    col_width = in_ref.shape[2] // col_tiles

    def store(source, target, first, part, width, parts):
        for piece in range(parts):

            @pl.when(part == piece)
            def _():
                for slot in range(slots):
                    block = list_ref[0, slot, position]
                    target[slot * tokens : (slot + 1) * tokens, first : first + width] = source[
                        block, :, piece * width : (piece + 1) * width
                    ]

    for shift in range(shifts):
        if by_shift:
            tile = lax.rem(position + shift, shifts)
            target = results[shift]
        else:
            tile = jnp.int32(shift)
            target = results[0].at[shift]
        store(out_ref, target, 0, tile // col_tiles, row_width, row_tiles)
        store(in_ref, target, row_width, lax.rem(tile, col_tiles), col_width, col_tiles)


def whole(array):
    return pl.BlockSpec(array.shape, lambda *i: (0,) * len(array.shape))


def pack_tokens(cand_out, cand_in, slot_blocks, row_tiles, col_tiles, shifts, by_shift):
    lists = jnp.swapaxes(slot_blocks, 1, 2)
    rows = slot_blocks.shape[2] * cand_out.shape[1]
    width = cand_out.shape[2] // row_tiles + cand_in.shape[2] // col_tiles
    if by_shift:
        shapes = [(rows, width)] * shifts
    else:
        shapes = [(shifts, rows, width)]
    results = [jax.ShapeDtypeStruct(shape, cand_out.dtype) for shape in shapes]
    return pl.pallas_call(
        functools.partial(
            pack_kernel,
            row_tiles=row_tiles,
            col_tiles=col_tiles,
            shifts=shifts,
            by_shift=by_shift,
        ),
        grid=(1,),
        in_specs=[pl.BlockSpec(memory_space=pltpu.SMEM), whole(cand_out), whole(cand_in)],
        out_specs=[whole(result) for result in results],
        out_shape=results,
    )(lists, cand_out, cand_in)


class Factors:
    def __init__(self, left_ref, right_ref, height, cols, row_tiles, col_tiles):
        position = lax.axis_index("cand")
        self.left_ref, self.right_ref = left_ref, right_ref
        self.height, self.cols = height, cols
        self.row_start = (position // col_tiles) * (left_ref.shape[2] // row_tiles)
        self.split = right_ref.shape[2] != cols
        self.col_start = lax.rem(position, col_tiles) * cols

    def left(self, query, block):
        start = pl.multiple_of(self.row_start + block * self.height, 128)
        rows = self.left_ref[query, :, pl.ds(start, self.height)]
        return rows.astype(jnp.float32).T.astype(jnp.bfloat16)

    def right(self, query, begin, end):
        if not self.split:
            return self.right_ref[query, :, begin:end]
        start = pl.multiple_of(self.col_start + begin, 128)
        return self.right_ref[query, :, pl.ds(start, end - begin)]


def spans(cols):
    return [(begin, min(begin + PIECE, cols)) for begin in range(0, cols, PIECE)]


def damped_inverse(lam_ref, begin, end):
    return 1.0 / (lam_ref[0, :, begin:end].astype(jnp.float32) + DAMPING)


def ahead_kernel(lam_ref, left_ref, right_ref, stored_ref, *, row_tiles, col_tiles):
    queries, height, cols = stored_ref.shape
    factors = Factors(left_ref, right_ref, height, cols, row_tiles, col_tiles)
    lefts = [factors.left(q, pl.program_id(0)) for q in range(queries)]
    for begin, end in spans(cols):
        inverse = damped_inverse(lam_ref, begin, end)
        for q in range(queries):
            outer = jnp.dot(
                lefts[q], factors.right(q, begin, end), preferred_element_type=jnp.float32
            )
            stored_ref[q, :, begin:end] = (outer * inverse).astype(jnp.bfloat16)


def score_kernel(lam_ref, left_ref, right_ref, *refs, ahead, tokens, results, row_tiles, col_tiles):
    token_refs, refs = refs[:results], refs[results:]
    stored_ref = None
    if ahead:
        stored_ref, refs = refs[0], refs[1:]
    score_refs, (acc_ref, token_buf) = refs[:results], refs[results:]
    queries, height, cols = left_ref.shape[0], lam_ref.shape[1], lam_ref.shape[2]
    step = pl.program_id(0)
    row_width = token_buf.shape[1]

    @pl.when(step == 0)
    def _():
        acc_ref[...] = jnp.zeros_like(acc_ref)
        start = 0
        for ref in token_refs:
            token_buf[start : start + ref.shape[0], :] = ref[:, :row_width]
            start += ref.shape[0]

    def token_rows(block):
        return token_buf[:, pl.ds(pl.multiple_of(block * height, 128), height)]

    factors = Factors(left_ref, right_ref, height, cols, row_tiles, col_tiles)
    lefts = [factors.left(q, step + ahead) for q in range(queries)]
    rows = token_rows(step + ahead)
    extra = []
    if ahead:
        for item in range(stored_ref.shape[0]):
            index = step * stored_ref.shape[0] + item
            extra.append((item, lax.rem(index, queries), token_rows(index // queries)))
    waiting = []

    def contract():
        q, begin, end, precond = waiting.pop(0)
        acc_ref[q, :, begin:end] += jnp.dot(rows, precond, preferred_element_type=jnp.float32)

    for begin, end in spans(cols):
        inverse = damped_inverse(lam_ref, begin, end)
        for q in range(queries):
            outer = jnp.dot(
                lefts[q], factors.right(q, begin, end), preferred_element_type=jnp.float32
            )
            if len(waiting) >= BEHIND:
                contract()
            waiting.append((q, begin, end, (outer * inverse).astype(jnp.bfloat16)))
        for item, query, block_rows in extra:
            acc_ref[query, :, begin:end] += jnp.dot(
                block_rows, stored_ref[item, :, begin:end], preferred_element_type=jnp.float32
            )
    while waiting:
        contract()

    @pl.when(step == pl.num_programs(0) - 1)
    def _():
        start = 0
        for ref, score_ref in zip(token_refs, score_refs):
            stop = start + ref.shape[0]
            inside = ref[:, row_width:].astype(jnp.float32)
            for q in range(queries):
                score_ref[q, :] = jnp.sum(acc_ref[q, start:stop, :] * inside, axis=1)
            start = stop


def pick(total, unit, limit):
    best = total
    if total % unit == 0:
        for size in range(unit, min(total, limit) + 1, unit):
            if total % size == 0:
                best = size
    return best


def blocks_ahead(steps, queries):
    for ahead in range(1, steps // 2 + 1):
        if (ahead * queries) % (steps - ahead) == 0:
            return ahead
    return 0


def tile_scores(lam, query_out, query_in, received, row_tiles, col_tiles):
    rows, cols = lam.shape[1:]
    queries, depth = query_in.shape[:2]
    tokens = sum(part.shape[0] for part in received)
    height = pick(rows, 128, 256)
    steps = rows // height
    ahead = blocks_ahead(steps, queries)
    if cols % 128:
        col_part = lax.rem(lax.axis_index("cand"), col_tiles)
        query_in = lax.dynamic_slice_in_dim(query_in, col_part * cols, cols, 2)
    tiles = dict(row_tiles=row_tiles, col_tiles=col_tiles)
    operands = [lam, query_out, query_in, *received]
    specs = [
        pl.BlockSpec((1, height, cols), lambda i: (0, i + ahead, 0)),
        *[whole(array) for array in operands[1:]],
    ]
    if ahead:
        stored = pl.pallas_call(
            functools.partial(ahead_kernel, **tiles),
            grid=(ahead,),
            in_specs=[pl.BlockSpec((1, height, cols), lambda i: (0, i, 0)), *specs[1:3]],
            out_specs=pl.BlockSpec((queries, height, cols), lambda i: (i, 0, 0)),
            out_shape=jax.ShapeDtypeStruct((ahead * queries, height, cols), jnp.bfloat16),
            compiler_params=pltpu.CompilerParams(vmem_limit_bytes=GRANT_AHEAD),
            cost_estimate=pl.CostEstimate(
                flops=2 * queries * ahead * height * cols * 256,
                bytes_accessed=ahead * height * cols * 2 * (queries + 1),
                transcendentals=ahead * height * cols,
            ),
        )(*operands[:3])
        per = ahead * queries // (steps - ahead)
        operands.append(stored)
        specs.append(pl.BlockSpec((per, height, cols), lambda i: (i, 0, 0)))
    results = [jax.ShapeDtypeStruct((queries, part.shape[0]), jnp.float32) for part in received]
    return pl.pallas_call(
        functools.partial(score_kernel, ahead=ahead, tokens=tokens, results=len(results), **tiles),
        grid=(steps - ahead,),
        in_specs=specs,
        out_specs=[whole(result) for result in results],
        out_shape=results,
        scratch_shapes=[
            pltpu.VMEM((queries, tokens, cols), jnp.float32),
            pltpu.VMEM((tokens, rows), jnp.bfloat16),
        ],
        compiler_params=pltpu.CompilerParams(vmem_limit_bytes=GRANT_MAIN),
        cost_estimate=pl.CostEstimate(
            flops=2 * queries * rows * cols * 512,
            bytes_accessed=2 * rows * cols,
            transcendentals=rows * cols,
        ),
    )(*operands)


def exchange(array):
    return lax.all_to_all(array, "cand", split_axis=0, concat_axis=0, tiled=True)


def shifted(array, shift, devices):
    pairs = [(device, (device + shift) % devices) for device in range(devices)]
    return lax.ppermute(array, "cand", pairs)


def body(cand_out, cand_in, query_out, query_in, eigenvalues, slot_blocks, live_counts):
    tile_count = lax.axis_size("cand")
    row_tiles = min(8, max(2, tile_count // 8))
    col_tiles = tile_count // row_tiles
    tokens = cand_out.shape[1]
    slot_count = slot_blocks.shape[2]
    queries = query_out.shape[0]
    by_shift = tile_count <= MAX_SHIFTS

    packed = pack_tokens(
        cand_out, cand_in, slot_blocks, row_tiles, col_tiles, tile_count, by_shift
    )
    if by_shift:
        received = [packed[0]] + [
            shifted(packed[shift], shift, tile_count) for shift in range(1, tile_count)
        ]
    else:
        received = [exchange(packed[0]).reshape(-1, packed[0].shape[2])]
    parts = tile_scores(eigenvalues, query_out, query_in, received, row_tiles, col_tiles)
    if by_shift:
        total = parts[0]
        for shift in range(1, tile_count):
            total = total + shifted(parts[shift], -shift, tile_count)
    else:
        split = jnp.moveaxis(parts[0].reshape(queries, tile_count, -1), 1, 0)
        total = jnp.sum(exchange(split), axis=0)
    scores = total.reshape(queries, slot_count, tokens).sum(axis=2)
    position = lax.axis_index("cand")
    own_live = lax.dynamic_index_in_dim(live_counts[0], position, 0, keepdims=False)
    used = jnp.arange(slot_count, dtype=jnp.int32) < own_live
    return jnp.where(used[None], scores, 0.0)[:, None, :]


def solution(mesh):
    return jax.shard_map(
        body,
        mesh=mesh,
        in_specs=(
            P(("parts", "cand"), None, None),
            P(("parts", "cand"), None, None),
            P(("parts", "query"), None, None),
            P(("parts", "query"), None, None),
            P("cand", None, None),
            P(("parts", "query"), None, None),
            P(("parts", "query"), None),
        ),
        out_specs=P(("parts", "query"), "cand", None),
        check_vma=False,
    )
```

time: 105 us -> 84 us (0.80)
  local copies, waits for them, and re-layouts: 10.1 us -> 2.92 us
  starting transfers between devices: 14.8 us -> 9.3 us
  waiting for transfers between devices: 8.67 us -> 5.39 us
  other arithmetic: 3.93 us -> 1.38 us
  Pallas kernels: 66.6 us -> 64.7 us
    all_to_all x3 -> x0, starting transfers between devices: 14.8 us -> none  [the longest x1 6.35 us: body(): lax.all_to_all(out_parts, 'cand', split_axis=0, concat_axis=0, tiled=True)]
    ppermute x0 -> x6, starting transfers between devices: none -> 9.3 us  [shifted(): return lax.ppermute(array, 'cand', pairs)]
    all_to_all x3 -> x0, waiting for transfers between devices: 8.67 us -> none  [the longest x1 4.92 us: body(): lax.all_to_all(jnp.moveaxis(totals, 1, 0), 'cand', split_axis=0, concat_a...]
    ppermute x0 -> x6, waiting for transfers between devices: none -> 5.39 us  [shifted(): return lax.ppermute(array, 'cand', pairs)]
    gather x2 -> x0, local copies, waits for them, and re-layouts: 3.25 us -> none  [the longest x1 1.72 us: body(): chosen_in = jnp.take(cand_in, own_slots, axis=0, mode='clip')]
    reduce_sum x3 -> x1, other arithmetic: 2.58 us -> 0.09 us  [body(): scores = total.reshape(queries, slot_count, tokens).sum(axis=2)]
    pallas_call x1 -> x3, Pallas kernels: 66.6 us -> 64.7 us  [the longest x1 47.2 us: tile_scores(): pl.pallas_call(functools.partial(score_kernel, ahead=ahead, tokens=tokens...]
    dynamic_slice x3 -> x0, local copies, waits for them, and re-layouts: 1.79 us -> none  [the longest x1 0.96 us: body(): lax.dynamic_index_in_dim(slot_blocks[0], position, 0, keepdims=False)]
  transfers between devices with their start and end apart: 3 -> 6, of which waited for: 2 -> 3; matrix products, arithmetic and copies ran while one was open for 6% -> 1% of each run, Pallas kernels for 64% -> 18%
where the time goes in v3:
time: 84 us; the launch traced here: 83.8 us
  Pallas kernels  64.7 us (77%)
  starting transfers between devices  9.3 us (11%)
  waiting for transfers between devices  5.39 us (6%)
  local copies, waits for them, and re-layouts  2.92 us (3%)
  other arithmetic  1.38 us (2%)
    pallas_call x1, Pallas kernels, tile_scores(): pl.pallas_call(functools.partial(score_kernel, ahead=ahead, tokens=tokens...  47.2 us
    pallas_call x1, Pallas kernels, tile_scores(): pl.pallas_call(functools.partial(ahead_kernel, **tiles), grid=(ahead,), i...  15.4 us
    ppermute x6, starting transfers between devices, shifted(): return lax.ppermute(array, 'cand', pairs)  9.3 us
    ppermute x6, waiting for transfers between devices, shifted(): return lax.ppermute(array, 'cand', pairs)  5.39 us
    pallas_call x1, Pallas kernels, pack_tokens(): pl.pallas_call(functools.partial(pack_kernel, row_tiles=row_tiles, col_ti...  2.2 us
    unnamed x12, local copies, waits for them, and re-layouts  2.15 us
  transfers between devices with their start and end apart: 6, of which 3 were waited for; matrix products, arithmetic and copies ran while one was open for 1% of the time, Pallas kernels for 18%

profile of v3, /device:TPU:0, one launch (start us, length us, event | category | flops | bytes accessed | tf_op | source)
XLA Modules:
  0.0 83.8 jit_solution(12502209938159274291)
XLA Ops:
  0.0 0.0 copy-start
  0.0 0.0 copy-start.4
  0.0 2.2 %shard_map.73 = (bf16[8,9472]{1,0:T(8,128)(2,1)}, bf16[8,9472]{1,0:T(8,128)(2,1)}, bf16[8,9472]{1,0:T(8,128)(2,1)}, bf16[8,9472]{1,0:T(8,128)(2,1)}) custom-call(s32[1,2,4]{2,1,0:T(2,128)} %bitcast.4, bf16[3,4,5120]{2,1,0:T(4,128)(2,1)} %out_ref.1, bf16[3,4,13824]{2,1,0:T(4,128)(2,1)} %in_ref.1), custom_call_target="tpu_custom_call" | custom-call | tf_op jit(solution)/shard_map/pallas_call | solution.py:62
  2.2 3.1 %collective-permute-start = (bf16[8,9472]{1,0:T(8,128)(2,1)}, bf16[8,9472]{1,0:T(8,128)(2,1)S(1)}, u32[]{:S(2)}, u32[]{:S(2)}) collective-permute-start(bf16[8,9472]{1,0:T(8,128)(2,1)} %get-tuple-element.14), channel_id=1, source_target_pairs={{0,4},{4,8},{8,12},{12,0},{1,5},{5,9},{9,13},{13,1},{2,6},{6,10},{... | collective-permute-start | bytes 454664 | tf_op jit(solution)/shard_map/ppermute | solution.py:256
  5.3 2.6 %collective-permute-start.1 = (bf16[8,9472]{1,0:T(8,128)(2,1)}, bf16[8,9472]{1,0:T(8,128)(2,1)S(1)}, u32[]{:S(2)}, u32[]{:S(2)}) collective-permute-start(bf16[8,9472]{1,0:T(8,128)(2,1)} %get-tuple-element.15), channel_id=1, source_target_pairs={{0,8},{4,12},{8,0},{12,4},{1,9},{5,13},{9,1},{13,5},{2,10},{6,14},... | collective-permute-start | bytes 454664 | tf_op jit(solution)/shard_map/ppermute | solution.py:256
  7.8 1.3 %collective-permute-start.2 = (bf16[8,9472]{1,0:T(8,128)(2,1)}, bf16[8,9472]{1,0:T(8,128)(2,1)S(1)}, u32[]{:S(2)}, u32[]{:S(2)}) collective-permute-start(bf16[8,9472]{1,0:T(8,128)(2,1)} %get-tuple-element.16), channel_id=1, source_target_pairs={{0,12},{4,0},{8,4},{12,8},{1,13},{5,1},{9,5},{13,9},{2,14},{6,2},{... | collective-permute-start | bytes 454664 | tf_op jit(solution)/shard_map/ppermute | solution.py:256
  9.2 0.0 copy-start.1
  9.2 1.2 %copy-done.1 = bf16[4,8,13824]{2,1,0:T(8,128)(2,1)S(1)} copy-done((bf16[4,8,13824]{2,1,0:T(8,128)(2,1)S(1)}, bf16[4,8,13824]{2,1,0:T(8,128)(2,1)}, u32[]{:S(2)}) %copy-start.1) | copy-done | bytes 884760
  10.4 0.0 copy-start.3
  10.4 1.0 %copy-done.3 = bf16[4,8,5120]{2,1,0:T(8,128)(2,1)S(1)} copy-done((bf16[4,8,5120]{2,1,0:T(8,128)(2,1)S(1)}, bf16[4,8,5120]{2,1,0:T(8,128)(2,1)}, u32[]{:S(2)}) %copy-start.3) | copy-done | bytes 327704
  11.3 0.0 copy-start.2
  11.3 15.4 %shard_map.74.refs_4_ = bf16[8,256,6912]{2,1,0:T(8,128)(2,1)} custom-call(bf16[1,2560,6912]{2,1,0:T(8,128)(2,1)} %lam_ref.3, bf16[4,8,5120]{2,1,0:T(8,128)(2,1)S(1)} %copy-done.3, bf16[4,8,13824]{2,1,0:T(8,128)(2,1)S(1)} %copy-done.1), custom_call_target="tpu_custom_call" | custom-call | flops 7247757312 | bytes 35389440 | tf_op jit(solution)/shard_map/pallas_call | solution.py:214
  26.7 0.0 copy-done
  26.7 0.6 constant_dynamic-slice_fusion
  27.3 0.6 iota_compare_fusion
  27.9 0.0 collective-permute-done.refs_1_
  27.9 0.0 collective-permute-done.1.refs_2_
  28.0 0.0 collective-permute-done.2.refs_3_
  28.0 0.0 copy-done.4
  28.0 0.0 copy-done.2
  28.0 0.0 copy-done.5
  28.0 47.2 %shard_map.75 = (f32[4,8]{1,0:T(4,128)S(1)}, f32[4,8]{1,0:T(4,128)S(1)}, f32[4,8]{1,0:T(4,128)S(1)}, f32[4,8]{1,0:T(4,128)S(1)}) custom-call(bf16[1,2560,6912]{2,1,0:T(8,128)(2,1)} %lam_ref.3, bf16[4,8,5120]{2,1,0:T(8,128)(2,1)S(1)} %copy-done.4, bf16[4,8,13824]{2,1,0:T(8,128)(2,1)S(1)} %copy-done.2, bf16[8,9472]{1,0:T(8,128)(2,1)S(1)} %copy-done.5, ...), custom_call_target="tpu_custom_call" | custom-call | flops 72477573120 | bytes 35389440 | tf_op jit(solution)/shard_map/pallas_call | solution.py:231
  75.1 0.6 collective-permute-start.3
  75.8 1.7 %collective-permute-start.4 = (f32[4,8]{1,0:T(4,128)S(1)}, f32[4,8]{1,0:T(4,128)S(1)}, u32[]{:S(2)}, u32[]{:S(2)}) collective-permute-start(f32[4,8]{1,0:T(4,128)S(1)} %get-tuple-element.19), channel_id=1, source_target_pairs={{0,8},{4,12},{8,0},{12,4},{1,9},{5,13},{9,1},{13,5},{2,10},{6,14},... | collective-permute-start | bytes 392 | tf_op jit(solution)/shard_map/ppermute | solution.py:256
  77.5 0.0 collective-permute-start.5
  77.5 1.3 %collective-permute-done.3 = f32[4,8]{1,0:T(4,128)S(1)} collective-permute-done((f32[4,8]{1,0:T(4,128)S(1)}, f32[4,8]{1,0:T(4,128)S(1)}, u32[]{:S(2)}, u32[]{:S(2)}) %collective-permute-start.3) | collective-permute-done | bytes 160 | tf_op jit(solution)/shard_map/ppermute | solution.py:256
  78.8 1.5 %collective-permute-done.4 = f32[4,8]{1,0:T(4,128)S(1)} collective-permute-done((f32[4,8]{1,0:T(4,128)S(1)}, f32[4,8]{1,0:T(4,128)S(1)}, u32[]{:S(2)}, u32[]{:S(2)}) %collective-permute-start.4) | collective-permute-done | bytes 160 | tf_op jit(solution)/shard_map/ppermute | solution.py:256
  80.3 2.6 %collective-permute-done.5 = f32[4,8]{1,0:T(4,128)S(1)} collective-permute-done((f32[4,8]{1,0:T(4,128)S(1)}, f32[4,8]{1,0:T(4,128)S(1)}, u32[]{:S(2)}, u32[]{:S(2)}) %collective-permute-start.5) | collective-permute-done | bytes 160 | tf_op jit(solution)/shard_map/ppermute | solution.py:256
  82.8 0.1 reshape.34
  82.9 0.1 reduce_sum.11
  83.0 0.1 copy.8
  83.1 0.6 bitcast_select_fusion
  (2 shorter events, 0.0 us)
Async XLA Ops:
  0.0 26.7 %copy-start = (s32[1,4]{1,0:T(1,128)S(1)}, s32[1,4]{1,0:T(1,128)}, u32[]{:S(2)}) copy-start(s32[1,4]{1,0:T(1,128)} %param.13) | copy-start | bytes 52
  0.0 28.0 %copy-start.4 = (bf16[4,8,5120]{2,1,0:T(8,128)(2,1)S(1)}, bf16[4,8,5120]{2,1,0:T(8,128)(2,1)}, u32[]{:S(2)}) copy-start(bf16[4,8,5120]{2,1,0:T(8,128)(2,1)} %left_ref.3) | copy-start | bytes 983044
  2.2 25.7 %collective-permute-start = (bf16[8,9472]{1,0:T(8,128)(2,1)}, bf16[8,9472]{1,0:T(8,128)(2,1)S(1)}, u32[]{:S(2)}, u32[]{:S(2)}) collective-permute-start(bf16[8,9472]{1,0:T(8,128)(2,1)} %get-tuple-element.14), channel_id=1, source_target_pairs={{0,4},{4,8},{8,12},{12,0},{1,5},{5,9},{9,13},{13,1},{2,6},{6,10},{... | collective-permute-start | bytes 454664 | tf_op jit(solution)/shard_map/ppermute | solution.py:256
  5.3 22.7 %collective-permute-start.1 = (bf16[8,9472]{1,0:T(8,128)(2,1)}, bf16[8,9472]{1,0:T(8,128)(2,1)S(1)}, u32[]{:S(2)}, u32[]{:S(2)}) collective-permute-start(bf16[8,9472]{1,0:T(8,128)(2,1)} %get-tuple-element.15), channel_id=1, source_target_pairs={{0,8},{4,12},{8,0},{12,4},{1,9},{5,13},{9,1},{13,5},{2,10},{6,14},... | collective-permute-start | bytes 454664 | tf_op jit(solution)/shard_map/ppermute | solution.py:256
  7.8 20.1 %collective-permute-start.2 = (bf16[8,9472]{1,0:T(8,128)(2,1)}, bf16[8,9472]{1,0:T(8,128)(2,1)S(1)}, u32[]{:S(2)}, u32[]{:S(2)}) collective-permute-start(bf16[8,9472]{1,0:T(8,128)(2,1)} %get-tuple-element.16), channel_id=1, source_target_pairs={{0,12},{4,0},{8,4},{12,8},{1,13},{5,1},{9,5},{13,9},{2,14},{6,2},{... | collective-permute-start | bytes 454664 | tf_op jit(solution)/shard_map/ppermute | solution.py:256
  9.2 1.2 %copy-start.1 = (bf16[4,8,13824]{2,1,0:T(8,128)(2,1)S(1)}, bf16[4,8,13824]{2,1,0:T(8,128)(2,1)}, u32[]{:S(2)}) copy-start(bf16[4,8,13824]{2,1,0:T(8,128)(2,1)} %right_ref.3) | copy-start | bytes 2654212
  10.4 1.0 %copy-start.3 = (bf16[4,8,5120]{2,1,0:T(8,128)(2,1)S(1)}, bf16[4,8,5120]{2,1,0:T(8,128)(2,1)}, u32[]{:S(2)}) copy-start(bf16[4,8,5120]{2,1,0:T(8,128)(2,1)} %left_ref.3) | copy-start | bytes 983044
  11.3 16.6 %copy-start.2 = (bf16[4,8,13824]{2,1,0:T(8,128)(2,1)S(1)}, bf16[4,8,13824]{2,1,0:T(8,128)(2,1)}, u32[]{:S(2)}) copy-start(bf16[4,8,13824]{2,1,0:T(8,128)(2,1)} %right_ref.3) | copy-start | bytes 2654212
  11.3 16.6 %copy-start.5 = (bf16[8,9472]{1,0:T(8,128)(2,1)S(1)}, bf16[8,9472]{1,0:T(8,128)(2,1)}, u32[]{:S(2)}) copy-start(bf16[8,9472]{1,0:T(8,128)(2,1)} %get-tuple-element.13.refs_0_) | copy-start | bytes 454660
  75.1 3.6 %collective-permute-start.3 = (f32[4,8]{1,0:T(4,128)S(1)}, f32[4,8]{1,0:T(4,128)S(1)}, u32[]{:S(2)}, u32[]{:S(2)}) collective-permute-start(f32[4,8]{1,0:T(4,128)S(1)} %get-tuple-element.18), channel_id=1, source_target_pairs={{0,12},{4,0},{8,4},{12,8},{1,13},{5,1},{9,5},{13,9},{2,14},{6,2},{... | collective-permute-start | bytes 392 | tf_op jit(solution)/shard_map/ppermute | solution.py:256
  75.8 4.5 %collective-permute-start.4 = (f32[4,8]{1,0:T(4,128)S(1)}, f32[4,8]{1,0:T(4,128)S(1)}, u32[]{:S(2)}, u32[]{:S(2)}) collective-permute-start(f32[4,8]{1,0:T(4,128)S(1)} %get-tuple-element.19), channel_id=1, source_target_pairs={{0,8},{4,12},{8,0},{12,4},{1,9},{5,13},{9,1},{13,5},{2,10},{6,14},... | collective-permute-start | bytes 392 | tf_op jit(solution)/shard_map/ppermute | solution.py:256
  77.5 5.4 %collective-permute-start.5 = (f32[4,8]{1,0:T(4,128)S(1)}, f32[4,8]{1,0:T(4,128)S(1)}, u32[]{:S(2)}, u32[]{:S(2)}) collective-permute-start(f32[4,8]{1,0:T(4,128)S(1)} %get-tuple-element.20), channel_id=1, source_target_pairs={{0,4},{4,8},{8,12},{12,0},{1,5},{5,9},{9,13},{13,1},{2,6},{6,10},{... | collective-permute-start | bytes 392 | tf_op jit(solution)/shard_map/ppermute | solution.py:256

commit v4 on v3

v4 whole, which is shorter than its diff:
```python
import functools

import jax
import jax.numpy as jnp
from jax import lax
from jax.experimental import pallas as pl
from jax.experimental.pallas import tpu as pltpu
from jax.sharding import PartitionSpec as P

DAMPING = 0.05
PIECE = 512
BEHIND = 2
MAX_SHIFTS = 8
GRANT_PACK = 8 << 20


def pack_kernel(list_ref, out_ref, in_ref, *results, row_tiles, col_tiles, shifts, by_shift):
    position = lax.axis_index("cand")
    slots = list_ref.shape[1]
    tokens = out_ref.shape[1]
    row_width = out_ref.shape[2] // row_tiles
    col_width = in_ref.shape[2] // col_tiles

    def store(source, target, part, width, parts):
        for piece in range(parts):

            @pl.when(part == piece)
            def _():
                for slot in range(slots):
                    block = list_ref[0, slot, position]
                    target[slot * tokens : (slot + 1) * tokens, :] = source[
                        block, :, piece * width : (piece + 1) * width
                    ]

    for shift in range(shifts):
        if by_shift:
            tile = lax.rem(position + shift, shifts)
            targets = results[shift], results[shifts + shift]
        else:
            tile = jnp.int32(shift)
            targets = results[0].at[shift], results[1].at[shift]
        store(out_ref, targets[0], tile // col_tiles, row_width, row_tiles)
        store(in_ref, targets[1], lax.rem(tile, col_tiles), col_width, col_tiles)


def in_hbm(array):
    return pltpu.with_memory_space_constraint(array, pltpu.HBM)


def whole(array):
    return pl.BlockSpec(array.shape, lambda *i: (0,) * len(array.shape))


def pack_tokens(cand_out, cand_in, slot_blocks, row_tiles, col_tiles, shifts, by_shift):
    lists = jnp.swapaxes(slot_blocks, 1, 2)
    rows = slot_blocks.shape[2] * cand_out.shape[1]
    widths = cand_out.shape[2] // row_tiles, cand_in.shape[2] // col_tiles
    if by_shift:
        shapes = [(rows, width) for width in widths for _ in range(shifts)]
    else:
        shapes = [(shifts, rows, width) for width in widths]
    results = [jax.ShapeDtypeStruct(shape, cand_out.dtype) for shape in shapes]
    return pl.pallas_call(
        functools.partial(
            pack_kernel,
            row_tiles=row_tiles,
            col_tiles=col_tiles,
            shifts=shifts,
            by_shift=by_shift,
        ),
        grid=(1,),
        in_specs=[pl.BlockSpec(memory_space=pltpu.SMEM), whole(cand_out), whole(cand_in)],
        out_specs=[whole(result) for result in results],
        out_shape=results,
        compiler_params=pltpu.CompilerParams(vmem_limit_bytes=GRANT_PACK),
    )(in_hbm(lists), in_hbm(cand_out), in_hbm(cand_in))


class Factors:
    def __init__(self, left_ref, right_ref, height, cols, row_tiles, col_tiles):
        position = lax.axis_index("cand")
        self.left_ref, self.right_ref = left_ref, right_ref
        self.height, self.cols = height, cols
        self.row_start = (position // col_tiles) * (left_ref.shape[2] // row_tiles)
        self.split = right_ref.shape[2] != cols
        self.col_start = lax.rem(position, col_tiles) * cols

    def left(self, query, block):
        start = pl.multiple_of(self.row_start + block * self.height, 128)
        rows = self.left_ref[query, :, pl.ds(start, self.height)]
        return rows.astype(jnp.float32).T.astype(jnp.bfloat16)

    def right(self, query, begin, end):
        if not self.split:
            return self.right_ref[query, :, begin:end]
        start = pl.multiple_of(self.col_start + begin, 128)
        return self.right_ref[query, :, pl.ds(start, end - begin)]


def map_kernel(lam_ref, left_ref, right_ref, *refs, row_tiles, col_tiles):
    token_refs, acc_ref, token_buf = refs[:-2], refs[-2], refs[-1]
    queries, height, cols = left_ref.shape[0], lam_ref.shape[1], lam_ref.shape[2]
    step = pl.program_id(0)

    @pl.when(step == 0)
    def _():
        acc_ref[...] = jnp.zeros_like(acc_ref)
        start = 0
        for ref in token_refs:
            token_buf[start : start + ref.shape[0], :] = ref[...]
            start += ref.shape[0]

    factors = Factors(left_ref, right_ref, height, cols, row_tiles, col_tiles)
    lefts = [factors.left(q, step) for q in range(queries)]
    rows = token_buf[:, pl.ds(pl.multiple_of(step * height, 128), height)]
    waiting = []

    def contract():
        q, begin, end, precond = waiting.pop(0)
        acc_ref[q, :, begin:end] += jnp.dot(rows, precond, preferred_element_type=jnp.float32)

    for begin in range(0, cols, PIECE):
        end = min(begin + PIECE, cols)
        inverse = 1.0 / (lam_ref[0, :, begin:end].astype(jnp.float32) + DAMPING)
        for q in range(queries):
            outer = jnp.dot(
                lefts[q], factors.right(q, begin, end), preferred_element_type=jnp.float32
            )
            if len(waiting) >= BEHIND:
                contract()
            waiting.append((q, begin, end, (outer * inverse).astype(jnp.bfloat16)))
    while waiting:
        contract()


def pick(total, unit, limit):
    best = total
    if total % unit == 0:
        for size in range(unit, min(total, limit) + 1, unit):
            if total % size == 0:
                best = size
    return best


def map_tokens(lam, query_out, query_in, out_tokens, row_tiles, col_tiles):
    rows, cols = lam.shape[1:]
    queries, depth = query_in.shape[:2]
    tokens = sum(part.shape[0] for part in out_tokens)
    height = pick(rows, 128, 256)
    if cols % 128:
        col_part = lax.rem(lax.axis_index("cand"), col_tiles)
        query_in = lax.dynamic_slice_in_dim(query_in, col_part * cols, cols, 2)
    grant = (16 << 20) + 4 * queries * tokens * cols + 4 * height * cols
    resident = pl.BlockSpec(memory_space=pltpu.VMEM)
    return pl.pallas_call(
        functools.partial(map_kernel, row_tiles=row_tiles, col_tiles=col_tiles),
        grid=(rows // height,),
        in_specs=[
            pl.BlockSpec((1, height, cols), lambda i: (0, i, 0)),
            whole(query_out),
            whole(query_in),
            *[resident] * len(out_tokens),
        ],
        out_specs=resident,
        out_shape=jax.ShapeDtypeStruct((queries, tokens, cols), jnp.float32),
        scratch_shapes=[pltpu.VMEM((tokens, rows), jnp.bfloat16)],
        compiler_params=pltpu.CompilerParams(vmem_limit_bytes=grant),
        cost_estimate=pl.CostEstimate(
            flops=2 * queries * rows * cols * 512,
            bytes_accessed=2 * rows * cols,
            transcendentals=rows * cols,
        ),
    )(lam, in_hbm(query_out), in_hbm(query_in), *out_tokens)


def fold_kernel(live_ref, mapped_ref, *refs, sources, per_slot):
    half = len(refs) // 2
    position = lax.axis_index("cand")
    start = 0
    for shift, (in_ref, score_ref) in enumerate(zip(refs[:half], refs[half:])):
        stop = start + in_ref.shape[0]
        inside = in_ref[...].astype(jnp.float32)
        for q in range(mapped_ref.shape[0]):
            score_ref[q, :] = jnp.sum(mapped_ref[q, start:stop, :] * inside, axis=1)
        start = stop
        if half == sources:
            live = live_ref[0, lax.rem(position + sources - shift, sources)]
            slot = lax.broadcasted_iota(jnp.int32, score_ref.shape, 1) // per_slot
            score_ref[...] = jnp.where(slot < live, score_ref[...], 0.0)


def fold_tokens(live_counts, mapped, in_tokens, per_slot):
    queries, tokens, cols = mapped.shape
    sources = live_counts.shape[1]
    grant = min((8 << 20) + 12 * queries * tokens * cols, 60 << 20)
    resident = pl.BlockSpec(memory_space=pltpu.VMEM)
    results = [jax.ShapeDtypeStruct((queries, part.shape[0]), jnp.float32) for part in in_tokens]
    return pl.pallas_call(
        functools.partial(fold_kernel, sources=sources, per_slot=per_slot),
        in_specs=[pl.BlockSpec(memory_space=pltpu.SMEM)] + [resident] * (1 + len(in_tokens)),
        out_specs=[resident] * len(results),
        out_shape=results,
        compiler_params=pltpu.CompilerParams(vmem_limit_bytes=grant),
    )(in_hbm(live_counts), mapped, *in_tokens)


def exchange(array):
    return lax.all_to_all(array, "cand", split_axis=0, concat_axis=0, tiled=True)


def shifted(array, shift, devices):
    pairs = [(device, (device + shift) % devices) for device in range(devices)]
    return lax.ppermute(array, "cand", pairs)


def body(cand_out, cand_in, query_out, query_in, eigenvalues, slot_blocks, live_counts):
    tile_count = lax.axis_size("cand")
    row_tiles = min(8, max(2, tile_count // 8))
    col_tiles = tile_count // row_tiles
    tokens = cand_out.shape[1]
    slot_count = slot_blocks.shape[2]
    queries = query_out.shape[0]
    by_shift = tile_count <= MAX_SHIFTS

    packed = pack_tokens(
        cand_out, cand_in, slot_blocks, row_tiles, col_tiles, tile_count, by_shift
    )
    if by_shift:
        out_tokens, in_tokens = [
            [group[0]] + [shifted(group[s], s, tile_count) for s in range(1, tile_count)]
            for group in (packed[:tile_count], packed[tile_count:])
        ]
    else:
        out_tokens, in_tokens = [
            [exchange(group).reshape(-1, group.shape[2])] for group in packed
        ]
    mapped = map_tokens(eigenvalues, query_out, query_in, out_tokens, row_tiles, col_tiles)
    parts = fold_tokens(live_counts, mapped, in_tokens, tokens)
    if by_shift:
        total = parts[0]
        for shift in range(1, tile_count):
            total = total + shifted(parts[shift], -shift, tile_count)
        return total.reshape(queries, 1, slot_count, tokens).sum(axis=3)
    split = jnp.moveaxis(parts[0].reshape(queries, tile_count, -1), 1, 0)
    total = jnp.sum(exchange(split), axis=0)
    scores = total.reshape(queries, slot_count, tokens).sum(axis=2)
    position = lax.axis_index("cand")
    own_live = lax.dynamic_index_in_dim(live_counts[0], position, 0, keepdims=False)
    used = jnp.arange(slot_count, dtype=jnp.int32) < own_live
    return jnp.where(used[None], scores, 0.0)[:, None, :]


def solution(mesh):
    return jax.shard_map(
        body,
        mesh=mesh,
        in_specs=(
            P(("parts", "cand"), None, None),
            P(("parts", "cand"), None, None),
            P(("parts", "query"), None, None),
            P(("parts", "query"), None, None),
            P("cand", None, None),
            P(("parts", "query"), None, None),
            P(("parts", "query"), None),
        ),
        out_specs=P(("parts", "query"), "cand", None),
        check_vma=False,
    )
```

time: 84 us -> 71.5 us (0.85)
  Pallas kernels: 64.7 us -> 51.7 us
  starting transfers between devices: 9.3 us -> 14.9 us
  local copies, waits for them, and re-layouts: 2.92 us -> 0.74 us
  waiting for transfers between devices: 5.39 us -> 3.85 us
  other arithmetic: 1.38 us -> 0.1 us
    pallas_call x2, Pallas kernels: 62.5 us -> 50.4 us  [the longest x1 49.4 us: map_tokens(): pl.pallas_call(functools.partial(map_kernel, row_tiles=row_tiles, col_til...]
    ppermute x6 -> x9, starting transfers between devices: 9.3 us -> 14.9 us  [shifted(): return lax.ppermute(array, 'cand', pairs)]
    unnamed x12 -> x0, local copies, waits for them, and re-layouts: 2.15 us -> none
    ppermute x6 -> x9, waiting for transfers between devices: 5.39 us -> 3.85 us  [shifted(): return lax.ppermute(array, 'cand', pairs)]
    pallas_call x1, Pallas kernels: 2.2 us -> 1.34 us  [pack_tokens(): pl.pallas_call(functools.partial(pack_kernel, row_tiles=row_tiles, col_ti...]
  transfers between devices with their start and end apart: 6 -> 9, of which waited for: 3 -> 2; matrix products, arithmetic and copies ran while one was open for 1% -> 0% of each run, Pallas kernels for 18% -> 69%
where the time goes in v4:
time: 71.5 us; the launch traced here: 71.4 us
  Pallas kernels  51.7 us (72%)
  starting transfers between devices  14.9 us (21%)
  waiting for transfers between devices  3.85 us (5%)
  local copies, waits for them, and re-layouts  0.74 us (1%)
    pallas_call x1, Pallas kernels, map_tokens(): pl.pallas_call(functools.partial(map_kernel, row_tiles=row_tiles, col_til...  49.4 us
    ppermute x9, starting transfers between devices, shifted(): return lax.ppermute(array, 'cand', pairs)  14.9 us
    ppermute x9, waiting for transfers between devices, shifted(): return lax.ppermute(array, 'cand', pairs)  3.85 us
  transfers between devices with their start and end apart: 9, of which 2 were waited for; matrix products, arithmetic and copies ran while one was open for 0% of the time, Pallas kernels for 69%

profile of v4, /device:TPU:0, one launch (start us, length us, event | category | flops | bytes accessed | tf_op | source)
XLA Modules:
  0.0 71.4 jit_solution(1744522423163542361)
XLA Ops:
  0.0 1.3 %shard_map.73 = (bf16[8,2560]{1,0:T(8,128)(2,1)S(1)}, bf16[8,2560]{1,0:T(8,128)(2,1)S(1)}, bf16[8,2560]{1,0:T(8,128)(2,1)S(1)}, bf16[8,2560]{1,0:T(8,128)(2,1)S(...) custom-call(s32[1,2,4]{2,1,0:T(2,128)} %bitcast.2, ...), custom_call_target="tpu_custom_call" | custom-call | tf_op jit(solution)/shard_map/pallas_call | solution.py:63
  1.3 3.1 %collective-permute-start = (bf16[8,2560]{1,0:T(8,128)(2,1)S(1)}, bf16[8,2560]{1,0:T(8,128)(2,1)S(1)}, u32[]{:S(2)}, u32[]{:S(2)}) collective-permute-start(bf16[8,2560]{1,0:T(8,128)(2,1)S(1)} %get-tuple-element.18), channel_id=1, source_target_pairs={{0,4},{4,8},{8,12},{12,0},{1,5},{5,9},{9,13},{13,1},{2,6},{6,10},{... | collective-permute-start | bytes 122888 | tf_op jit(solution)/shard_map/ppermute | solution.py:213
  4.5 2.6 %collective-permute-start.1 = (bf16[8,2560]{1,0:T(8,128)(2,1)S(1)}, bf16[8,2560]{1,0:T(8,128)(2,1)S(1)}, u32[]{:S(2)}, u32[]{:S(2)}) collective-permute-start(bf16[8,2560]{1,0:T(8,128)(2,1)S(1)} %get-tuple-element.19), channel_id=1, source_target_pairs={{0,8},{4,12},{8,0},{12,4},{1,9},{5,13},{9,1},{13,5},{2,10},{6,14},... | collective-permute-start | bytes 122888 | tf_op jit(solution)/shard_map/ppermute | solution.py:213
  7.0 1.3 %collective-permute-start.2 = (bf16[8,2560]{1,0:T(8,128)(2,1)S(1)}, bf16[8,2560]{1,0:T(8,128)(2,1)S(1)}, u32[]{:S(2)}, u32[]{:S(2)}) collective-permute-start(bf16[8,2560]{1,0:T(8,128)(2,1)S(1)} %get-tuple-element.20), channel_id=1, source_target_pairs={{0,12},{4,0},{8,4},{12,8},{1,13},{5,1},{9,5},{13,9},{2,14},{6,2},{... | collective-permute-start | bytes 122888 | tf_op jit(solution)/shard_map/ppermute | solution.py:213
  8.4 0.7 collective-permute-start.3
  9.1 0.3 collective-permute-start.4
  9.4 0.0 collective-permute-done.refs_1_
  9.4 2.8 %collective-permute-start.5 = (bf16[8,6912]{1,0:T(8,128)(2,1)S(1)}, bf16[8,6912]{1,0:T(8,128)(2,1)S(1)}, u32[]{:S(2)}, u32[]{:S(2)}) collective-permute-start(bf16[8,6912]{1,0:T(8,128)(2,1)S(1)} %get-tuple-element.24), channel_id=1, source_target_pairs={{0,12},{4,0},{8,4},{12,8},{1,13},{5,1},{9,5},{13,9},{2,14},{6,2},{... | collective-permute-start | bytes 331784 | tf_op jit(solution)/shard_map/ppermute | solution.py:213
  12.2 0.0 collective-permute-done.1.refs_2_
  12.2 0.0 collective-permute-done.2.refs_3_
  12.2 49.4 %shard_map.74.mapped_ref = f32[4,32,6912]{2,1,0:T(8,128)S(1)} custom-call(bf16[1,2560,6912]{2,1,0:T(8,128)(2,1)} %lam_ref.1, bf16[4,8,5120]{2,1,0:T(8,128)(2,1)} %left_ref.1, bf16[4,8,13824]{2,1,0:T(8,128)(2,1)} %right_ref.1, bf16[8,2560]{1,0:T(8,128)(2,1)S(1)} %get-tuple-element.17.refs_0_, bf16[8,2560]{1,0:T(8,128)(2,1)S(1)} %collective-permute-done.refs_1_, ...), custom_call_target="tpu_custom_call" | custom-call | flops 72477573120 | bytes 35389440 | tf_op jit(solution)/shard_map/pallas_call | solution.py:155
  61.6 0.0 collective-permute-done.3.refs_1_
  61.6 0.0 collective-permute-done.4.refs_2_
  61.6 0.0 collective-permute-done.5.refs_3_
  61.6 1.0 %shard_map.75 = (f32[4,8]{1,0:T(4,128)S(1)}, f32[4,8]{1,0:T(4,128)S(1)}, f32[4,8]{1,0:T(4,128)S(1)}, f32[4,8]{1,0:T(4,128)S(1)}) custom-call(s32[1,4]{1,0:T(1,128)} %live_ref.1, f32[4,32,6912]{2,1,0:T(8,128)S(1)} %shard_map.74.mapped_ref, bf16[8,6912]{1,0:T(8,128)(2,1)S(1)} %get-tuple-element.21.refs_0_, bf16[8,6912]{1,0:T(8,128)(2,1)S(1)} %collective-permute-done.3.refs_1_, ...), custom_call_target="tpu_custom_call" | custom-call | tf_op jit(solution)/shard_map/pallas_call | solution.py:198
  62.7 2.5 %collective-permute-start.6 = (f32[4,8]{1,0:T(4,128)S(1)}, f32[4,8]{1,0:T(4,128)S(1)}, u32[]{:S(2)}, u32[]{:S(2)}) collective-permute-start(f32[4,8]{1,0:T(4,128)S(1)} %get-tuple-element.26), channel_id=1, source_target_pairs={{0,12},{4,0},{8,4},{12,8},{1,13},{5,1},{9,5},{13,9},{2,14},{6,2},{... | collective-permute-start | bytes 392 | tf_op jit(solution)/shard_map/ppermute | solution.py:213
  65.2 0.0 collective-permute-start.7
  65.2 1.5 %collective-permute-start.8 = (f32[4,8]{1,0:T(4,128)S(1)}, f32[4,8]{1,0:T(4,128)S(1)}, u32[]{:S(2)}, u32[]{:S(2)}) collective-permute-start(f32[4,8]{1,0:T(4,128)S(1)} %get-tuple-element.28), channel_id=1, source_target_pairs={{0,4},{4,8},{8,12},{12,0},{1,5},{5,9},{9,13},{13,1},{2,6},{6,10},{... | collective-permute-start | bytes 392 | tf_op jit(solution)/shard_map/ppermute | solution.py:213
  66.7 0.0 collective-permute-done.6
  66.7 2.9 %collective-permute-done.7 = f32[4,8]{1,0:T(4,128)S(1)} collective-permute-done((f32[4,8]{1,0:T(4,128)S(1)}, f32[4,8]{1,0:T(4,128)S(1)}, u32[]{:S(2)}, u32[]{:S(2)}) %collective-permute-start.7) | collective-permute-done | bytes 160 | tf_op jit(solution)/shard_map/ppermute | solution.py:213
  69.6 0.9 %collective-permute-done.8 = f32[4,8]{1,0:T(4,128)S(1)} collective-permute-done((f32[4,8]{1,0:T(4,128)S(1)}, f32[4,8]{1,0:T(4,128)S(1)}, u32[]{:S(2)}, u32[]{:S(2)}) %collective-permute-start.8) | collective-permute-done | bytes 160 | tf_op jit(solution)/shard_map/ppermute | solution.py:213
  70.6 0.1 reshape.4
  70.6 0.1 reduce_sum.11
  70.7 0.7 copy.8
  (1 shorter events, 0.0 us)
Async XLA Ops:
  1.3 8.1 %collective-permute-start = (bf16[8,2560]{1,0:T(8,128)(2,1)S(1)}, bf16[8,2560]{1,0:T(8,128)(2,1)S(1)}, u32[]{:S(2)}, u32[]{:S(2)}) collective-permute-start(bf16[8,2560]{1,0:T(8,128)(2,1)S(1)} %get-tuple-element.18), channel_id=1, source_target_pairs={{0,4},{4,8},{8,12},{12,0},{1,5},{5,9},{9,13},{13,1},{2,6},{6,10},{... | collective-permute-start | bytes 122888 | tf_op jit(solution)/shard_map/ppermute | solution.py:213
  4.5 7.8 %collective-permute-start.1 = (bf16[8,2560]{1,0:T(8,128)(2,1)S(1)}, bf16[8,2560]{1,0:T(8,128)(2,1)S(1)}, u32[]{:S(2)}, u32[]{:S(2)}) collective-permute-start(bf16[8,2560]{1,0:T(8,128)(2,1)S(1)} %get-tuple-element.19), channel_id=1, source_target_pairs={{0,8},{4,12},{8,0},{12,4},{1,9},{5,13},{9,1},{13,5},{2,10},{6,14},... | collective-permute-start | bytes 122888 | tf_op jit(solution)/shard_map/ppermute | solution.py:213
  7.0 5.2 %collective-permute-start.2 = (bf16[8,2560]{1,0:T(8,128)(2,1)S(1)}, bf16[8,2560]{1,0:T(8,128)(2,1)S(1)}, u32[]{:S(2)}, u32[]{:S(2)}) collective-permute-start(bf16[8,2560]{1,0:T(8,128)(2,1)S(1)} %get-tuple-element.20), channel_id=1, source_target_pairs={{0,12},{4,0},{8,4},{12,8},{1,13},{5,1},{9,5},{13,9},{2,14},{6,2},{... | collective-permute-start | bytes 122888 | tf_op jit(solution)/shard_map/ppermute | solution.py:213
  8.4 53.2 %collective-permute-start.3 = (bf16[8,6912]{1,0:T(8,128)(2,1)S(1)}, bf16[8,6912]{1,0:T(8,128)(2,1)S(1)}, u32[]{:S(2)}, u32[]{:S(2)}) collective-permute-start(bf16[8,6912]{1,0:T(8,128)(2,1)S(1)} %get-tuple-element.22), channel_id=1, source_target_pairs={{0,4},{4,8},{8,12},{12,0},{1,5},{5,9},{9,13},{13,1},{2,6},{6,10},{... | collective-permute-start | bytes 331784 | tf_op jit(solution)/shard_map/ppermute | solution.py:213
  9.1 52.5 %collective-permute-start.4 = (bf16[8,6912]{1,0:T(8,128)(2,1)S(1)}, bf16[8,6912]{1,0:T(8,128)(2,1)S(1)}, u32[]{:S(2)}, u32[]{:S(2)}) collective-permute-start(bf16[8,6912]{1,0:T(8,128)(2,1)S(1)} %get-tuple-element.23), channel_id=1, source_target_pairs={{0,8},{4,12},{8,0},{12,4},{1,9},{5,13},{9,1},{13,5},{2,10},{6,14},... | collective-permute-start | bytes 331784 | tf_op jit(solution)/shard_map/ppermute | solution.py:213
  9.4 52.2 %collective-permute-start.5 = (bf16[8,6912]{1,0:T(8,128)(2,1)S(1)}, bf16[8,6912]{1,0:T(8,128)(2,1)S(1)}, u32[]{:S(2)}, u32[]{:S(2)}) collective-permute-start(bf16[8,6912]{1,0:T(8,128)(2,1)S(1)} %get-tuple-element.24), channel_id=1, source_target_pairs={{0,12},{4,0},{8,4},{12,8},{1,13},{5,1},{9,5},{13,9},{2,14},{6,2},{... | collective-permute-start | bytes 331784 | tf_op jit(solution)/shard_map/ppermute | solution.py:213
  62.7 4.0 %collective-permute-start.6 = (f32[4,8]{1,0:T(4,128)S(1)}, f32[4,8]{1,0:T(4,128)S(1)}, u32[]{:S(2)}, u32[]{:S(2)}) collective-permute-start(f32[4,8]{1,0:T(4,128)S(1)} %get-tuple-element.26), channel_id=1, source_target_pairs={{0,12},{4,0},{8,4},{12,8},{1,13},{5,1},{9,5},{13,9},{2,14},{6,2},{... | collective-permute-start | bytes 392 | tf_op jit(solution)/shard_map/ppermute | solution.py:213
  65.2 4.5 %collective-permute-start.7 = (f32[4,8]{1,0:T(4,128)S(1)}, f32[4,8]{1,0:T(4,128)S(1)}, u32[]{:S(2)}, u32[]{:S(2)}) collective-permute-start(f32[4,8]{1,0:T(4,128)S(1)} %get-tuple-element.27), channel_id=1, source_target_pairs={{0,8},{4,12},{8,0},{12,4},{1,9},{5,13},{9,1},{13,5},{2,10},{6,14},... | collective-permute-start | bytes 392 | tf_op jit(solution)/shard_map/ppermute | solution.py:213
  65.2 5.4 %collective-permute-start.8 = (f32[4,8]{1,0:T(4,128)S(1)}, f32[4,8]{1,0:T(4,128)S(1)}, u32[]{:S(2)}, u32[]{:S(2)}) collective-permute-start(f32[4,8]{1,0:T(4,128)S(1)} %get-tuple-element.28), channel_id=1, source_target_pairs={{0,4},{4,8},{8,12},{12,0},{1,5},{5,9},{9,13},{13,1},{2,6},{6,10},{... | collective-permute-start | bytes 392 | tf_op jit(solution)/shard_map/ppermute | solution.py:213

commit v5 on v4

--- a/solution.py
+++ b/solution.py
@@ -10,11 +10,10 @@
 DAMPING = 0.05
 PIECE = 512
 BEHIND = 2
-MAX_SHIFTS = 8
 GRANT_PACK = 8 << 20
 
 
-def pack_kernel(list_ref, out_ref, in_ref, *results, row_tiles, col_tiles, shifts, by_shift):
+def pack_kernel(list_ref, out_ref, in_ref, *results, row_tiles, col_tiles, shifts, paired):
     position = lax.axis_index("cand")
     slots = list_ref.shape[1]
     tokens = out_ref.shape[1]
@@ -33,8 +32,8 @@
                     ]
 
     for shift in range(shifts):
-        if by_shift:
-            tile = lax.rem(position + shift, shifts)
+        if paired:
+            tile = lax.bitwise_xor(position, jnp.int32(shift))
             targets = results[shift], results[shifts + shift]
         else:
             tile = jnp.int32(shift)
@@ -51,11 +50,11 @@
     return pl.BlockSpec(array.shape, lambda *i: (0,) * len(array.shape))
 
 
-def pack_tokens(cand_out, cand_in, slot_blocks, row_tiles, col_tiles, shifts, by_shift):
+def pack_tokens(cand_out, cand_in, slot_blocks, row_tiles, col_tiles, shifts, paired):
     lists = jnp.swapaxes(slot_blocks, 1, 2)
     rows = slot_blocks.shape[2] * cand_out.shape[1]
     widths = cand_out.shape[2] // row_tiles, cand_in.shape[2] // col_tiles
-    if by_shift:
+    if paired:
         shapes = [(rows, width) for width in widths for _ in range(shifts)]
     else:
         shapes = [(shifts, rows, width) for width in widths]
@@ -66,7 +65,7 @@
             row_tiles=row_tiles,
             col_tiles=col_tiles,
             shifts=shifts,
-            by_shift=by_shift,
+            paired=paired,
         ),
         grid=(1,),
         in_specs=[pl.BlockSpec(memory_space=pltpu.SMEM), whole(cand_out), whole(cand_in)],
@@ -173,30 +172,45 @@
     )(lam, in_hbm(query_out), in_hbm(query_in), *out_tokens)
 
 
-def fold_kernel(live_ref, mapped_ref, *refs, sources, per_slot):
-    half = len(refs) // 2
+def fold_kernel(live_ref, mapped_ref, *refs, paired, per_slot):
+    queries = mapped_ref.shape[0]
+    token_refs = refs[:-2] if paired else refs[:-1]
     position = lax.axis_index("cand")
     start = 0
-    for shift, (in_ref, score_ref) in enumerate(zip(refs[:half], refs[half:])):
-        stop = start + in_ref.shape[0]
+    for index, in_ref in enumerate(token_refs):
+        rows = in_ref.shape[0]
         inside = in_ref[...].astype(jnp.float32)
-        for q in range(mapped_ref.shape[0]):
-            score_ref[q, :] = jnp.sum(mapped_ref[q, start:stop, :] * inside, axis=1)
-        start = stop
-        if half == sources:
-            live = live_ref[0, lax.rem(position + sources - shift, sources)]
-            slot = lax.broadcasted_iota(jnp.int32, score_ref.shape, 1) // per_slot
-            score_ref[...] = jnp.where(slot < live, score_ref[...], 0.0)
-
-
-def fold_tokens(live_counts, mapped, in_tokens, per_slot):
+        sums = [
+            jnp.sum(mapped_ref[q, start : start + rows, :] * inside, axis=1, keepdims=True)
+            for q in range(queries)
+        ]
+        start += rows
+        if not paired:
+            for q in range(queries):
+                refs[-1][q, :] = sums[q][:, 0]
+            continue
+        lane = lax.broadcasted_iota(jnp.int32, (rows, queries), 1)
+        table = sum(jnp.where(lane == q, sums[q], 0.0) for q in range(queries))
+        live = live_ref[0, lax.bitwise_xor(position, jnp.int32(index))]
+        half = len(token_refs) // 2
+        target = refs[-2 + index // half]
+        for slot in range(rows // per_slot):
+            part = table[slot * per_slot : (slot + 1) * per_slot]
+            total = jnp.sum(part, axis=0, keepdims=True)
+            target[index % half, slot : slot + 1, :] = jnp.where(slot < live, total, 0.0)
+
+
+def fold_tokens(live_counts, mapped, in_tokens, per_slot, paired):
     queries, tokens, cols = mapped.shape
-    sources = live_counts.shape[1]
     grant = min((8 << 20) + 12 * queries * tokens * cols, 60 << 20)
     resident = pl.BlockSpec(memory_space=pltpu.VMEM)
-    results = [jax.ShapeDtypeStruct((queries, part.shape[0]), jnp.float32) for part in in_tokens]
+    if paired:
+        shape = (len(in_tokens) // 2, in_tokens[0].shape[0] // per_slot, queries)
+        results = [jax.ShapeDtypeStruct(shape, jnp.float32)] * 2
+    else:
+        results = [jax.ShapeDtypeStruct((queries, tokens), jnp.float32)]
     return pl.pallas_call(
-        functools.partial(fold_kernel, sources=sources, per_slot=per_slot),
+        functools.partial(fold_kernel, paired=paired, per_slot=per_slot),
         in_specs=[pl.BlockSpec(memory_space=pltpu.SMEM)] + [resident] * (1 + len(in_tokens)),
         out_specs=[resident] * len(results),
         out_shape=results,
@@ -208,8 +222,8 @@
     return lax.all_to_all(array, "cand", split_axis=0, concat_axis=0, tiled=True)
 
 
-def shifted(array, shift, devices):
-    pairs = [(device, (device + shift) % devices) for device in range(devices)]
+def swapped(array, bit, devices):
+    pairs = [(device, device ^ bit) for device in range(devices)]
     return lax.ppermute(array, "cand", pairs)
 
 
@@ -220,14 +234,14 @@
     tokens = cand_out.shape[1]
     slot_count = slot_blocks.shape[2]
     queries = query_out.shape[0]
-    by_shift = tile_count <= MAX_SHIFTS
+    paired = tile_count in (2, 4, 8)
 
     packed = pack_tokens(
-        cand_out, cand_in, slot_blocks, row_tiles, col_tiles, tile_count, by_shift
+        cand_out, cand_in, slot_blocks, row_tiles, col_tiles, tile_count, paired
     )
-    if by_shift:
+    if paired:
         out_tokens, in_tokens = [
-            [group[0]] + [shifted(group[s], s, tile_count) for s in range(1, tile_count)]
+            [group[0]] + [swapped(group[s], s, tile_count) for s in range(1, tile_count)]
             for group in (packed[:tile_count], packed[tile_count:])
         ]
     else:
@@ -235,12 +249,16 @@
             [exchange(group).reshape(-1, group.shape[2])] for group in packed
         ]
     mapped = map_tokens(eigenvalues, query_out, query_in, out_tokens, row_tiles, col_tiles)
-    parts = fold_tokens(live_counts, mapped, in_tokens, tokens)
-    if by_shift:
-        total = parts[0]
-        for shift in range(1, tile_count):
-            total = total + shifted(parts[shift], -shift, tile_count)
-        return total.reshape(queries, 1, slot_count, tokens).sum(axis=3)
+    parts = fold_tokens(live_counts, mapped, in_tokens, tokens, paired)
+    if paired:
+        kept, sent = parts
+        bit = tile_count // 2
+        while True:
+            kept = kept + swapped(sent, bit, tile_count)
+            bit //= 2
+            if not bit:
+                return jnp.transpose(kept, (2, 0, 1))
+            kept, sent = kept[:bit], kept[bit:]
     split = jnp.moveaxis(parts[0].reshape(queries, tile_count, -1), 1, 0)
     total = jnp.sum(exchange(split), axis=0)
     scores = total.reshape(queries, slot_count, tokens).sum(axis=2)

time: 71.5 us -> 72.7 us (1.017)
  waiting for transfers between devices: 3.85 us -> 10 us
  starting transfers between devices: 14.9 us -> 10.2 us
  local copies, waits for them, and re-layouts: 0.74 us -> 0.01 us
    ppermute x9 -> x8, waiting for transfers between devices: 3.85 us -> 10 us  [swapped(): return lax.ppermute(array, 'cand', pairs)]
    ppermute x9 -> x8, starting transfers between devices: 14.9 us -> 10.2 us  [swapped(): return lax.ppermute(array, 'cand', pairs)]
  transfers between devices with their start and end apart: 9 -> 8, of which waited for: 2 -> 3; matrix products, arithmetic and copies ran while one was open for 0% -> 0% of each run, Pallas kernels for 69% -> 68%
where the time goes in v5:
time: 72.7 us; the launch traced here: 72.5 us
  Pallas kernels  51.8 us (71%)
  starting transfers between devices  10.2 us (14%)
  waiting for transfers between devices  10 us (14%)
    pallas_call x1, Pallas kernels, map_tokens(): pl.pallas_call(functools.partial(map_kernel, row_tiles=row_tiles, col_til...  49.3 us
    ppermute x8, starting transfers between devices, swapped(): return lax.ppermute(array, 'cand', pairs)  10.2 us
    ppermute x8, waiting for transfers between devices, swapped(): return lax.ppermute(array, 'cand', pairs)  10 us
  transfers between devices with their start and end apart: 8, of which 3 were waited for; matrix products, arithmetic and copies ran while one was open for 0% of the time, Pallas kernels for 68%

profile of v5, /device:TPU:0, one launch (start us, length us, event | category | flops | bytes accessed | tf_op | source)
XLA Modules:
  0.0 72.5 jit_solution(15253325724390256474)
XLA Ops:
  0.0 1.3 %shard_map.73 = (bf16[8,2560]{1,0:T(8,128)(2,1)S(1)}, bf16[8,2560]{1,0:T(8,128)(2,1)S(1)}, bf16[8,2560]{1,0:T(8,128)(2,1)S(1)}, bf16[8,2560]{1,0:T(8,128)(2,1)S(...) custom-call(s32[1,2,4]{2,1,0:T(2,128)} %bitcast.3, ...), custom_call_target="tpu_custom_call" | custom-call | tf_op jit(solution)/shard_map/pallas_call | solution.py:62
  1.3 3.1 %collective-permute-start = (bf16[8,2560]{1,0:T(8,128)(2,1)S(1)}, bf16[8,2560]{1,0:T(8,128)(2,1)S(1)}, u32[]{:S(2)}, u32[]{:S(2)}) collective-permute-start(bf16[8,2560]{1,0:T(8,128)(2,1)S(1)} %get-tuple-element.16), channel_id=1, source_target_pairs={{0,4},{4,0},{8,12},{12,8},{1,5},{5,1},{9,13},{13,9},{2,6},{6,2},{1... | collective-permute-start | bytes 122888 | tf_op jit(solution)/shard_map/ppermute | solution.py:227
  4.5 2.6 %collective-permute-start.1 = (bf16[8,2560]{1,0:T(8,128)(2,1)S(1)}, bf16[8,2560]{1,0:T(8,128)(2,1)S(1)}, u32[]{:S(2)}, u32[]{:S(2)}) collective-permute-start(bf16[8,2560]{1,0:T(8,128)(2,1)S(1)} %get-tuple-element.17), channel_id=1, source_target_pairs={{0,8},{4,12},{8,0},{12,4},{1,9},{5,13},{9,1},{13,5},{2,10},{6,14},... | collective-permute-start | bytes 122888 | tf_op jit(solution)/shard_map/ppermute | solution.py:227
  7.0 0.0 collective-permute-start.2
  7.0 0.9 %collective-permute-start.3 = (bf16[8,6912]{1,0:T(8,128)(2,1)S(1)}, bf16[8,6912]{1,0:T(8,128)(2,1)S(1)}, u32[]{:S(2)}, u32[]{:S(2)}) collective-permute-start(bf16[8,6912]{1,0:T(8,128)(2,1)S(1)} %get-tuple-element.20), channel_id=1, source_target_pairs={{0,4},{4,0},{8,12},{12,8},{1,5},{5,1},{9,13},{13,9},{2,6},{6,2},{1... | collective-permute-start | bytes 331784 | tf_op jit(solution)/shard_map/ppermute | solution.py:227
  7.9 3.5 %collective-permute-start.4 = (bf16[8,6912]{1,0:T(8,128)(2,1)S(1)}, bf16[8,6912]{1,0:T(8,128)(2,1)S(1)}, u32[]{:S(2)}, u32[]{:S(2)}) collective-permute-start(bf16[8,6912]{1,0:T(8,128)(2,1)S(1)} %get-tuple-element.21), channel_id=1, source_target_pairs={{0,8},{4,12},{8,0},{12,4},{1,9},{5,13},{9,1},{13,5},{2,10},{6,14},... | collective-permute-start | bytes 331784 | tf_op jit(solution)/shard_map/ppermute | solution.py:227
  11.4 0.0 collective-permute-done.refs_1_
  11.4 0.0 collective-permute-start.5
  11.4 0.0 collective-permute-done.1.refs_2_
  11.4 1.9 %collective-permute-done.2.refs_3_ = bf16[8,2560]{1,0:T(8,128)(2,1)S(1)} collective-permute-done((bf16[8,2560]{1,0:T(8,128)(2,1)S(1)}, bf16[8,2560]{1,0:T(8,128)(2,1)S(1)}, u32[]{:S(2)}, u32[]{:S(2)}) %collective-permute-start.2) | collective-permute-done | bytes 40992 | tf_op jit(solution)/shard_map/ppermute | solution.py:227
  13.4 49.3 %shard_map.74.mapped_ref = f32[4,32,6912]{2,1,0:T(8,128)S(1)} custom-call(bf16[1,2560,6912]{2,1,0:T(8,128)(2,1)} %lam_ref.1, bf16[4,8,5120]{2,1,0:T(8,128)(2,1)} %left_ref.1, bf16[4,8,13824]{2,1,0:T(8,128)(2,1)} %right_ref.1, bf16[8,2560]{1,0:T(8,128)(2,1)S(1)} %get-tuple-element.15.refs_0_, bf16[8,2560]{1,0:T(8,128)(2,1)S(1)} %collective-permute-done.refs_1_, ...), custom_call_target="tpu_custom_call" | custom-call | flops 72477573120 | bytes 35389440 | tf_op jit(solution)/shard_map/pallas_call | solution.py:154
  62.7 0.0 collective-permute-done.3.refs_1_
  62.7 0.0 collective-permute-done.4.refs_2_
  62.8 0.0 collective-permute-done.5.refs_3_
  62.8 1.1 %shard_map.75 = (f32[2,2,4]{2,1,0:T(2,128)S(1)}, f32[2,2,4]{2,1,0:T(2,128)S(1)}) custom-call(s32[1,4]{1,0:T(1,128)} %live_ref.1, f32[4,32,6912]{2,1,0:T(8,128)S(1)} %shard_map.74.mapped_ref, bf16[8,6912]{1,0:T(8,128)(2,1)S(1)} %get-tuple-element.19.refs_0_, bf16[8,6912]{1,0:T(8,128)(2,1)S(1)} %collective-permute-done.3.refs_1_, ...), custom_call_target="tpu_custom_call" | custom-call | tf_op jit(solution)/shard_map/pallas_call | solution.py:212
  63.8 0.1 collective-permute-start.6
  63.9 4.5 %collective-permute-done.6 = f32[2,2,4]{2,1,0:T(2,128)S(1)} collective-permute-done((f32[2,2,4]{2,1,0:T(2,128)S(1)}, f32[2,2,4]{2,1,0:T(2,128)S(1)}, u32[]{:S(2)}, u32[]{:S(2)}) %collective-permute-start.6) | collective-permute-done | bytes 96 | tf_op jit(solution)/shard_map/ppermute | solution.py:227
  68.4 0.0 collective-permute-start.7
  68.4 3.6 %collective-permute-done.7 = f32[1,2,4]{2,1,0:T(2,128)S(1)} collective-permute-done((f32[1,2,4]{2,1,0:T(2,128)S(1)}, f32[1,2,4]{2,1,0:T(2,128)S(1)}, u32[]{:S(2)}, u32[]{:S(2)}) %collective-permute-start.7) | collective-permute-done | bytes 64 | tf_op jit(solution)/shard_map/ppermute | solution.py:227
  72.0 0.6 fusion
  (2 shorter events, 0.0 us)
Async XLA Ops:
  1.3 10.1 %collective-permute-start = (bf16[8,2560]{1,0:T(8,128)(2,1)S(1)}, bf16[8,2560]{1,0:T(8,128)(2,1)S(1)}, u32[]{:S(2)}, u32[]{:S(2)}) collective-permute-start(bf16[8,2560]{1,0:T(8,128)(2,1)S(1)} %get-tuple-element.16), channel_id=1, source_target_pairs={{0,4},{4,0},{8,12},{12,8},{1,5},{5,1},{9,13},{13,9},{2,6},{6,2},{1... | collective-permute-start | bytes 122888 | tf_op jit(solution)/shard_map/ppermute | solution.py:227
  4.5 7.0 %collective-permute-start.1 = (bf16[8,2560]{1,0:T(8,128)(2,1)S(1)}, bf16[8,2560]{1,0:T(8,128)(2,1)S(1)}, u32[]{:S(2)}, u32[]{:S(2)}) collective-permute-start(bf16[8,2560]{1,0:T(8,128)(2,1)S(1)} %get-tuple-element.17), channel_id=1, source_target_pairs={{0,8},{4,12},{8,0},{12,4},{1,9},{5,13},{9,1},{13,5},{2,10},{6,14},... | collective-permute-start | bytes 122888 | tf_op jit(solution)/shard_map/ppermute | solution.py:227
  7.0 6.3 %collective-permute-start.2 = (bf16[8,2560]{1,0:T(8,128)(2,1)S(1)}, bf16[8,2560]{1,0:T(8,128)(2,1)S(1)}, u32[]{:S(2)}, u32[]{:S(2)}) collective-permute-start(bf16[8,2560]{1,0:T(8,128)(2,1)S(1)} %get-tuple-element.18), channel_id=1, source_target_pairs={{0,12},{4,8},{8,4},{12,0},{1,13},{5,9},{9,5},{13,1},{2,14},{6,10},... | collective-permute-start | bytes 122888 | tf_op jit(solution)/shard_map/ppermute | solution.py:227
  7.0 55.7 %collective-permute-start.3 = (bf16[8,6912]{1,0:T(8,128)(2,1)S(1)}, bf16[8,6912]{1,0:T(8,128)(2,1)S(1)}, u32[]{:S(2)}, u32[]{:S(2)}) collective-permute-start(bf16[8,6912]{1,0:T(8,128)(2,1)S(1)} %get-tuple-element.20), channel_id=1, source_target_pairs={{0,4},{4,0},{8,12},{12,8},{1,5},{5,1},{9,13},{13,9},{2,6},{6,2},{1... | collective-permute-start | bytes 331784 | tf_op jit(solution)/shard_map/ppermute | solution.py:227
  7.9 54.8 %collective-permute-start.4 = (bf16[8,6912]{1,0:T(8,128)(2,1)S(1)}, bf16[8,6912]{1,0:T(8,128)(2,1)S(1)}, u32[]{:S(2)}, u32[]{:S(2)}) collective-permute-start(bf16[8,6912]{1,0:T(8,128)(2,1)S(1)} %get-tuple-element.21), channel_id=1, source_target_pairs={{0,8},{4,12},{8,0},{12,4},{1,9},{5,13},{9,1},{13,5},{2,10},{6,14},... | collective-permute-start | bytes 331784 | tf_op jit(solution)/shard_map/ppermute | solution.py:227
  11.4 51.3 %collective-permute-start.5 = (bf16[8,6912]{1,0:T(8,128)(2,1)S(1)}, bf16[8,6912]{1,0:T(8,128)(2,1)S(1)}, u32[]{:S(2)}, u32[]{:S(2)}) collective-permute-start(bf16[8,6912]{1,0:T(8,128)(2,1)S(1)} %get-tuple-element.22), channel_id=1, source_target_pairs={{0,12},{4,8},{8,4},{12,0},{1,13},{5,9},{9,5},{13,1},{2,14},{6,10},... | collective-permute-start | bytes 331784 | tf_op jit(solution)/shard_map/ppermute | solution.py:227
  63.8 4.5 %collective-permute-start.6 = (f32[2,2,4]{2,1,0:T(2,128)S(1)}, f32[2,2,4]{2,1,0:T(2,128)S(1)}, u32[]{:S(2)}, u32[]{:S(2)}) collective-permute-start(f32[2,2,4]{2,1,0:T(2,128)S(1)} %get-tuple-element.24), channel_id=1, source_target_pairs={{0,8},{4,12},{8,0},{12,4},{1,9},{5,13},{9,1},{13,5},{2,10},{6,14},... | collective-permute-start | bytes 200 | tf_op jit(solution)/shard_map/ppermute | solution.py:227
  68.4 3.6 %collective-permute-start.7 = (f32[1,2,4]{2,1,0:T(2,128)S(1)}, f32[1,2,4]{2,1,0:T(2,128)S(1)}, u32[]{:S(2)}, u32[]{:S(2)}) collective-permute-start(f32[1,2,4]{2,1,0:T(2,128)S(1)} %slice.9), channel_id=1, source_target_pairs={{0,4},{4,0},{8,12},{12,8},{1,5},{5,1},{9,13},{13,9},{2,6},{6,2},{1... | collective-permute-start | bytes 104 | tf_op jit(solution)/shard_map/ppermute | solution.py:227

commit v6 on v4

--- a/solution.py
+++ b/solution.py
@@ -173,30 +173,45 @@
     )(lam, in_hbm(query_out), in_hbm(query_in), *out_tokens)
 
 
-def fold_kernel(live_ref, mapped_ref, *refs, sources, per_slot):
-    half = len(refs) // 2
+def fold_kernel(live_ref, mapped_ref, *refs, by_shift, per_slot):
+    queries = mapped_ref.shape[0]
+    token_refs = refs[: len(refs) // 2]
     position = lax.axis_index("cand")
     start = 0
-    for shift, (in_ref, score_ref) in enumerate(zip(refs[:half], refs[half:])):
-        stop = start + in_ref.shape[0]
+    for index, in_ref in enumerate(token_refs):
+        rows = in_ref.shape[0]
         inside = in_ref[...].astype(jnp.float32)
-        for q in range(mapped_ref.shape[0]):
-            score_ref[q, :] = jnp.sum(mapped_ref[q, start:stop, :] * inside, axis=1)
-        start = stop
-        if half == sources:
-            live = live_ref[0, lax.rem(position + sources - shift, sources)]
-            slot = lax.broadcasted_iota(jnp.int32, score_ref.shape, 1) // per_slot
-            score_ref[...] = jnp.where(slot < live, score_ref[...], 0.0)
-
-
-def fold_tokens(live_counts, mapped, in_tokens, per_slot):
+        sums = [
+            jnp.sum(mapped_ref[q, start : start + rows, :] * inside, axis=1, keepdims=True)
+            for q in range(queries)
+        ]
+        start += rows
+        if not by_shift:
+            for q in range(queries):
+                refs[-1][q, :] = sums[q][:, 0]
+            continue
+        lane = lax.broadcasted_iota(jnp.int32, (rows, queries), 1)
+        table = sum(jnp.where(lane == q, sums[q], 0.0) for q in range(queries))
+        sources = len(token_refs)
+        live = live_ref[0, lax.rem(position + sources - index, sources)]
+        target = refs[sources + index]
+        for slot in range(rows // per_slot):
+            part = table[slot * per_slot : (slot + 1) * per_slot]
+            total = jnp.sum(part, axis=0, keepdims=True)
+            target[slot : slot + 1, :] = jnp.where(slot < live, total, 0.0)
+
+
+def fold_tokens(live_counts, mapped, in_tokens, per_slot, by_shift):
     queries, tokens, cols = mapped.shape
-    sources = live_counts.shape[1]
     grant = min((8 << 20) + 12 * queries * tokens * cols, 60 << 20)
     resident = pl.BlockSpec(memory_space=pltpu.VMEM)
-    results = [jax.ShapeDtypeStruct((queries, part.shape[0]), jnp.float32) for part in in_tokens]
+    if by_shift:
+        shape = (in_tokens[0].shape[0] // per_slot, queries)
+        results = [jax.ShapeDtypeStruct(shape, jnp.float32)] * len(in_tokens)
+    else:
+        results = [jax.ShapeDtypeStruct((queries, tokens), jnp.float32)]
     return pl.pallas_call(
-        functools.partial(fold_kernel, sources=sources, per_slot=per_slot),
+        functools.partial(fold_kernel, by_shift=by_shift, per_slot=per_slot),
         in_specs=[pl.BlockSpec(memory_space=pltpu.SMEM)] + [resident] * (1 + len(in_tokens)),
         out_specs=[resident] * len(results),
         out_shape=results,
@@ -235,12 +250,12 @@
             [exchange(group).reshape(-1, group.shape[2])] for group in packed
         ]
     mapped = map_tokens(eigenvalues, query_out, query_in, out_tokens, row_tiles, col_tiles)
-    parts = fold_tokens(live_counts, mapped, in_tokens, tokens)
+    parts = fold_tokens(live_counts, mapped, in_tokens, tokens, by_shift)
     if by_shift:
         total = parts[0]
         for shift in range(1, tile_count):
             total = total + shifted(parts[shift], -shift, tile_count)
-        return total.reshape(queries, 1, slot_count, tokens).sum(axis=3)
+        return jnp.transpose(total[None], (2, 0, 1))
     split = jnp.moveaxis(parts[0].reshape(queries, tile_count, -1), 1, 0)
     total = jnp.sum(exchange(split), axis=0)
     scores = total.reshape(queries, slot_count, tokens).sum(axis=2)

time: 71.5 us -> 71.3 us (level)
  local copies, waits for them, and re-layouts: 0.74 us -> 0 us
where the time goes in v6:
time: 71.3 us; the launch traced here: 71.2 us
  Pallas kernels  51.8 us (73%)
  starting transfers between devices  15 us (21%)
  waiting for transfers between devices  3.84 us (5%)
    pallas_call x1, Pallas kernels, map_tokens(): pl.pallas_call(functools.partial(map_kernel, row_tiles=row_tiles, col_til...  49.4 us
    ppermute x9, starting transfers between devices, shifted(): return lax.ppermute(array, 'cand', pairs)  15 us
    ppermute x9, waiting for transfers between devices, shifted(): return lax.ppermute(array, 'cand', pairs)  3.84 us
  transfers between devices with their start and end apart: 9, of which 2 were waited for; matrix products, arithmetic and copies ran while one was open for 0% of the time, Pallas kernels for 69%

profile of v6, /device:TPU:0, one launch (start us, length us, event | category | flops | bytes accessed | tf_op | source)
XLA Modules:
  0.0 71.2 jit_solution(3130435751419972622)
XLA Ops:
  0.0 1.3 %shard_map.73 = (bf16[8,2560]{1,0:T(8,128)(2,1)S(1)}, bf16[8,2560]{1,0:T(8,128)(2,1)S(1)}, bf16[8,2560]{1,0:T(8,128)(2,1)S(1)}, bf16[8,2560]{1,0:T(8,128)(2,1)S(...) custom-call(s32[1,2,4]{2,1,0:T(2,128)} %bitcast.5, ...), custom_call_target="tpu_custom_call" | custom-call | tf_op jit(solution)/shard_map/pallas_call | solution.py:63
  1.3 3.1 %collective-permute-start = (bf16[8,2560]{1,0:T(8,128)(2,1)S(1)}, bf16[8,2560]{1,0:T(8,128)(2,1)S(1)}, u32[]{:S(2)}, u32[]{:S(2)}) collective-permute-start(bf16[8,2560]{1,0:T(8,128)(2,1)S(1)} %get-tuple-element.18), channel_id=1, source_target_pairs={{0,4},{4,8},{8,12},{12,0},{1,5},{5,9},{9,13},{13,1},{2,6},{6,10},{... | collective-permute-start | bytes 122888 | tf_op jit(solution)/shard_map/ppermute | solution.py:228
  4.5 2.6 %collective-permute-start.1 = (bf16[8,2560]{1,0:T(8,128)(2,1)S(1)}, bf16[8,2560]{1,0:T(8,128)(2,1)S(1)}, u32[]{:S(2)}, u32[]{:S(2)}) collective-permute-start(bf16[8,2560]{1,0:T(8,128)(2,1)S(1)} %get-tuple-element.19), channel_id=1, source_target_pairs={{0,8},{4,12},{8,0},{12,4},{1,9},{5,13},{9,1},{13,5},{2,10},{6,14},... | collective-permute-start | bytes 122888 | tf_op jit(solution)/shard_map/ppermute | solution.py:228
  7.0 1.3 %collective-permute-start.2 = (bf16[8,2560]{1,0:T(8,128)(2,1)S(1)}, bf16[8,2560]{1,0:T(8,128)(2,1)S(1)}, u32[]{:S(2)}, u32[]{:S(2)}) collective-permute-start(bf16[8,2560]{1,0:T(8,128)(2,1)S(1)} %get-tuple-element.20), channel_id=1, source_target_pairs={{0,12},{4,0},{8,4},{12,8},{1,13},{5,1},{9,5},{13,9},{2,14},{6,2},{... | collective-permute-start | bytes 122888 | tf_op jit(solution)/shard_map/ppermute | solution.py:228
  8.4 0.7 collective-permute-start.3
  9.1 0.3 collective-permute-start.4
  9.4 0.0 collective-permute-done.refs_1_
  9.4 2.8 %collective-permute-start.5 = (bf16[8,6912]{1,0:T(8,128)(2,1)S(1)}, bf16[8,6912]{1,0:T(8,128)(2,1)S(1)}, u32[]{:S(2)}, u32[]{:S(2)}) collective-permute-start(bf16[8,6912]{1,0:T(8,128)(2,1)S(1)} %get-tuple-element.24), channel_id=1, source_target_pairs={{0,12},{4,0},{8,4},{12,8},{1,13},{5,1},{9,5},{13,9},{2,14},{6,2},{... | collective-permute-start | bytes 331784 | tf_op jit(solution)/shard_map/ppermute | solution.py:228
  12.2 0.0 collective-permute-done.1.refs_2_
  12.2 0.0 collective-permute-done.2.refs_3_
  12.2 49.4 %shard_map.74.mapped_ref = f32[4,32,6912]{2,1,0:T(8,128)S(1)} custom-call(bf16[1,2560,6912]{2,1,0:T(8,128)(2,1)} %lam_ref.1, bf16[4,8,5120]{2,1,0:T(8,128)(2,1)} %left_ref.1, bf16[4,8,13824]{2,1,0:T(8,128)(2,1)} %right_ref.1, bf16[8,2560]{1,0:T(8,128)(2,1)S(1)} %get-tuple-element.17.refs_0_, bf16[8,2560]{1,0:T(8,128)(2,1)S(1)} %collective-permute-done.refs_1_, ...), custom_call_target="tpu_custom_call" | custom-call | flops 72477573120 | bytes 35389440 | tf_op jit(solution)/shard_map/pallas_call | solution.py:155
  61.6 0.0 collective-permute-done.3.refs_1_
  61.6 0.0 collective-permute-done.4.refs_2_
  61.6 0.0 collective-permute-done.5.refs_3_
  61.6 1.1 %shard_map.75 = (f32[2,4]{1,0:T(2,128)S(1)}, f32[2,4]{1,0:T(2,128)S(1)}, f32[2,4]{1,0:T(2,128)S(1)}, f32[2,4]{1,0:T(2,128)S(1)}) custom-call(s32[1,4]{1,0:T(1,128)} %live_ref.1, f32[4,32,6912]{2,1,0:T(8,128)S(1)} %shard_map.74.mapped_ref, bf16[8,6912]{1,0:T(8,128)(2,1)S(1)} %get-tuple-element.21.refs_0_, bf16[8,6912]{1,0:T(8,128)(2,1)S(1)} %collective-permute-done.3.refs_1_, ...), custom_call_target="tpu_custom_call" | custom-call | tf_op jit(solution)/shard_map/pallas_call | solution.py:213
  62.7 2.5 %collective-permute-start.6 = (f32[2,4]{1,0:T(2,128)S(1)}, f32[2,4]{1,0:T(2,128)S(1)}, u32[]{:S(2)}, u32[]{:S(2)}) collective-permute-start(f32[2,4]{1,0:T(2,128)S(1)} %get-tuple-element.26), channel_id=1, source_target_pairs={{0,12},{4,0},{8,4},{12,8},{1,13},{5,1},{9,5},{13,9},{2,14},{6,2},{... | collective-permute-start | bytes 104 | tf_op jit(solution)/shard_map/ppermute | solution.py:228
  65.2 0.0 collective-permute-start.7
  65.2 1.5 %collective-permute-start.8 = (f32[2,4]{1,0:T(2,128)S(1)}, f32[2,4]{1,0:T(2,128)S(1)}, u32[]{:S(2)}, u32[]{:S(2)}) collective-permute-start(f32[2,4]{1,0:T(2,128)S(1)} %get-tuple-element.28), channel_id=1, source_target_pairs={{0,4},{4,8},{8,12},{12,0},{1,5},{5,9},{9,13},{13,1},{2,6},{6,10},{... | collective-permute-start | bytes 104 | tf_op jit(solution)/shard_map/ppermute | solution.py:228
  66.8 0.0 collective-permute-done.6
  66.8 2.9 %collective-permute-done.7 = f32[2,4]{1,0:T(2,128)S(1)} collective-permute-done((f32[2,4]{1,0:T(2,128)S(1)}, f32[2,4]{1,0:T(2,128)S(1)}, u32[]{:S(2)}, u32[]{:S(2)}) %collective-permute-start.7) | collective-permute-done | bytes 64 | tf_op jit(solution)/shard_map/ppermute | solution.py:228
  69.7 0.9 %collective-permute-done.8 = f32[2,4]{1,0:T(2,128)S(1)} collective-permute-done((f32[2,4]{1,0:T(2,128)S(1)}, f32[2,4]{1,0:T(2,128)S(1)}, u32[]{:S(2)}, u32[]{:S(2)}) %collective-permute-start.8) | collective-permute-done | bytes 64 | tf_op jit(solution)/shard_map/ppermute | solution.py:228
  70.6 0.6 add_bitcast_fusion
Async XLA Ops:
  1.3 8.1 %collective-permute-start = (bf16[8,2560]{1,0:T(8,128)(2,1)S(1)}, bf16[8,2560]{1,0:T(8,128)(2,1)S(1)}, u32[]{:S(2)}, u32[]{:S(2)}) collective-permute-start(bf16[8,2560]{1,0:T(8,128)(2,1)S(1)} %get-tuple-element.18), channel_id=1, source_target_pairs={{0,4},{4,8},{8,12},{12,0},{1,5},{5,9},{9,13},{13,1},{2,6},{6,10},{... | collective-permute-start | bytes 122888 | tf_op jit(solution)/shard_map/ppermute | solution.py:228
  4.5 7.8 %collective-permute-start.1 = (bf16[8,2560]{1,0:T(8,128)(2,1)S(1)}, bf16[8,2560]{1,0:T(8,128)(2,1)S(1)}, u32[]{:S(2)}, u32[]{:S(2)}) collective-permute-start(bf16[8,2560]{1,0:T(8,128)(2,1)S(1)} %get-tuple-element.19), channel_id=1, source_target_pairs={{0,8},{4,12},{8,0},{12,4},{1,9},{5,13},{9,1},{13,5},{2,10},{6,14},... | collective-permute-start | bytes 122888 | tf_op jit(solution)/shard_map/ppermute | solution.py:228
  7.0 5.2 %collective-permute-start.2 = (bf16[8,2560]{1,0:T(8,128)(2,1)S(1)}, bf16[8,2560]{1,0:T(8,128)(2,1)S(1)}, u32[]{:S(2)}, u32[]{:S(2)}) collective-permute-start(bf16[8,2560]{1,0:T(8,128)(2,1)S(1)} %get-tuple-element.20), channel_id=1, source_target_pairs={{0,12},{4,0},{8,4},{12,8},{1,13},{5,1},{9,5},{13,9},{2,14},{6,2},{... | collective-permute-start | bytes 122888 | tf_op jit(solution)/shard_map/ppermute | solution.py:228
  8.4 53.2 %collective-permute-start.3 = (bf16[8,6912]{1,0:T(8,128)(2,1)S(1)}, bf16[8,6912]{1,0:T(8,128)(2,1)S(1)}, u32[]{:S(2)}, u32[]{:S(2)}) collective-permute-start(bf16[8,6912]{1,0:T(8,128)(2,1)S(1)} %get-tuple-element.22), channel_id=1, source_target_pairs={{0,4},{4,8},{8,12},{12,0},{1,5},{5,9},{9,13},{13,1},{2,6},{6,10},{... | collective-permute-start | bytes 331784 | tf_op jit(solution)/shard_map/ppermute | solution.py:228
  9.1 52.5 %collective-permute-start.4 = (bf16[8,6912]{1,0:T(8,128)(2,1)S(1)}, bf16[8,6912]{1,0:T(8,128)(2,1)S(1)}, u32[]{:S(2)}, u32[]{:S(2)}) collective-permute-start(bf16[8,6912]{1,0:T(8,128)(2,1)S(1)} %get-tuple-element.23), channel_id=1, source_target_pairs={{0,8},{4,12},{8,0},{12,4},{1,9},{5,13},{9,1},{13,5},{2,10},{6,14},... | collective-permute-start | bytes 331784 | tf_op jit(solution)/shard_map/ppermute | solution.py:228
  9.4 52.2 %collective-permute-start.5 = (bf16[8,6912]{1,0:T(8,128)(2,1)S(1)}, bf16[8,6912]{1,0:T(8,128)(2,1)S(1)}, u32[]{:S(2)}, u32[]{:S(2)}) collective-permute-start(bf16[8,6912]{1,0:T(8,128)(2,1)S(1)} %get-tuple-element.24), channel_id=1, source_target_pairs={{0,12},{4,0},{8,4},{12,8},{1,13},{5,1},{9,5},{13,9},{2,14},{6,2},{... | collective-permute-start | bytes 331784 | tf_op jit(solution)/shard_map/ppermute | solution.py:228
  62.7 4.1 %collective-permute-start.6 = (f32[2,4]{1,0:T(2,128)S(1)}, f32[2,4]{1,0:T(2,128)S(1)}, u32[]{:S(2)}, u32[]{:S(2)}) collective-permute-start(f32[2,4]{1,0:T(2,128)S(1)} %get-tuple-element.26), channel_id=1, source_target_pairs={{0,12},{4,0},{8,4},{12,8},{1,13},{5,1},{9,5},{13,9},{2,14},{6,2},{... | collective-permute-start | bytes 104 | tf_op jit(solution)/shard_map/ppermute | solution.py:228
  65.2 4.5 %collective-permute-start.7 = (f32[2,4]{1,0:T(2,128)S(1)}, f32[2,4]{1,0:T(2,128)S(1)}, u32[]{:S(2)}, u32[]{:S(2)}) collective-permute-start(f32[2,4]{1,0:T(2,128)S(1)} %get-tuple-element.27), channel_id=1, source_target_pairs={{0,8},{4,12},{8,0},{12,4},{1,9},{5,13},{9,1},{13,5},{2,10},{6,14},... | collective-permute-start | bytes 104 | tf_op jit(solution)/shard_map/ppermute | solution.py:228
  65.2 5.4 %collective-permute-start.8 = (f32[2,4]{1,0:T(2,128)S(1)}, f32[2,4]{1,0:T(2,128)S(1)}, u32[]{:S(2)}, u32[]{:S(2)}) collective-permute-start(f32[2,4]{1,0:T(2,128)S(1)} %get-tuple-element.28), channel_id=1, source_target_pairs={{0,4},{4,8},{8,12},{12,0},{1,5},{5,9},{9,13},{13,1},{2,6},{6,10},{... | collective-permute-start | bytes 104 | tf_op jit(solution)/shard_map/ppermute | solution.py:228

commit v7 on v6

--- a/solution.py
+++ b/solution.py
@@ -98,13 +98,14 @@
 
 
 def map_kernel(lam_ref, left_ref, right_ref, *refs, row_tiles, col_tiles):
-    token_refs, acc_ref, token_buf = refs[:-2], refs[-2], refs[-1]
+    token_refs, (acc_ref, token_buf, held) = refs[:-3], refs[-3:]
     queries, height, cols = left_ref.shape[0], lam_ref.shape[1], lam_ref.shape[2]
     step = pl.program_id(0)
 
     @pl.when(step == 0)
     def _():
         acc_ref[...] = jnp.zeros_like(acc_ref)
+        held[...] = jnp.zeros_like(held)
         start = 0
         for ref in token_refs:
             token_buf[start : start + ref.shape[0], :] = ref[...]
@@ -112,25 +113,40 @@
 
     factors = Factors(left_ref, right_ref, height, cols, row_tiles, col_tiles)
     lefts = [factors.left(q, step) for q in range(queries)]
-    rows = token_buf[:, pl.ds(pl.multiple_of(step * height, 128), height)]
-    waiting = []
+    behind = held.shape[0]
+    pieces = [(begin, min(begin + PIECE, cols)) for begin in range(0, cols, PIECE)]
+    begin, end = pieces[-1]
+
+    def token_rows(block):
+        return token_buf[:, pl.ds(pl.multiple_of(block * height, 128), height)]
+
+    rows, rows_before = token_rows(step), token_rows(jnp.maximum(step - 1, 0))
+    carried = range(queries - behind, queries)
+    waiting = [
+        (q, begin, end, rows_before, held[slot, :, : end - begin]) for slot, q in enumerate(carried)
+    ]
 
     def contract():
-        q, begin, end, precond = waiting.pop(0)
-        acc_ref[q, :, begin:end] += jnp.dot(rows, precond, preferred_element_type=jnp.float32)
-
-    for begin in range(0, cols, PIECE):
-        end = min(begin + PIECE, cols)
+        q, begin, end, mine, precond = waiting.pop(0)
+        acc_ref[q, :, begin:end] += jnp.dot(mine, precond, preferred_element_type=jnp.float32)
+
+    for begin, end in pieces:
         inverse = 1.0 / (lam_ref[0, :, begin:end].astype(jnp.float32) + DAMPING)
         for q in range(queries):
             outer = jnp.dot(
                 lefts[q], factors.right(q, begin, end), preferred_element_type=jnp.float32
             )
-            if len(waiting) >= BEHIND:
-                contract()
-            waiting.append((q, begin, end, (outer * inverse).astype(jnp.bfloat16)))
-    while waiting:
-        contract()
+            contract()
+            waiting.append((q, begin, end, rows, (outer * inverse).astype(jnp.bfloat16)))
+    for slot, item in enumerate(waiting):
+        held[slot, :, : end - begin] = item[-1]
+
+    @pl.when(step == pl.num_programs(0) - 1)
+    def _():
+        for slot, q in enumerate(carried):
+            acc_ref[q, :, begin:end] += jnp.dot(
+                rows, held[slot, :, : end - begin], preferred_element_type=jnp.float32
+            )
 
 
 def pick(total, unit, limit):
@@ -163,7 +179,10 @@
         ],
         out_specs=resident,
         out_shape=jax.ShapeDtypeStruct((queries, tokens, cols), jnp.float32),
-        scratch_shapes=[pltpu.VMEM((tokens, rows), jnp.bfloat16)],
+        scratch_shapes=[
+            pltpu.VMEM((tokens, rows), jnp.bfloat16),
+            pltpu.VMEM((min(BEHIND, queries), height, min(PIECE, cols)), jnp.bfloat16),
+        ],
         compiler_params=pltpu.CompilerParams(vmem_limit_bytes=grant),
         cost_estimate=pl.CostEstimate(
             flops=2 * queries * rows * cols * 512,

time: 71.3 us -> 70 us (0.982)
  Pallas kernels: 51.8 us -> 50.4 us
    pallas_call x1, Pallas kernels: 49.4 us -> 48 us  [map_tokens(): pl.pallas_call(functools.partial(map_kernel, row_tiles=row_tiles, col_til...]
where the time goes in v7:
time: 70 us; the launch traced here: 69.8 us
  Pallas kernels  50.4 us (72%)
  starting transfers between devices  15 us (21%)
  waiting for transfers between devices  3.84 us (5%)
    pallas_call x1, Pallas kernels, map_tokens(): pl.pallas_call(functools.partial(map_kernel, row_tiles=row_tiles, col_til...  48 us
    ppermute x9, starting transfers between devices, shifted(): return lax.ppermute(array, 'cand', pairs)  15 us
    ppermute x9, waiting for transfers between devices, shifted(): return lax.ppermute(array, 'cand', pairs)  3.84 us
  transfers between devices with their start and end apart: 9, of which 2 were waited for; matrix products, arithmetic and copies ran while one was open for 0% of the time, Pallas kernels for 69%

profile of v7, /device:TPU:0, one launch (start us, length us, event | category | flops | bytes accessed | tf_op | source)
XLA Modules:
  0.0 69.8 jit_solution(16450986449779017607)
XLA Ops:
  0.0 1.3 %shard_map.73 = (bf16[8,2560]{1,0:T(8,128)(2,1)S(1)}, bf16[8,2560]{1,0:T(8,128)(2,1)S(1)}, bf16[8,2560]{1,0:T(8,128)(2,1)S(1)}, bf16[8,2560]{1,0:T(8,128)(2,1)S(...) custom-call(s32[1,2,4]{2,1,0:T(2,128)} %bitcast.5, ...), custom_call_target="tpu_custom_call" | custom-call | tf_op jit(solution)/shard_map/pallas_call | solution.py:63
  1.3 3.1 %collective-permute-start = (bf16[8,2560]{1,0:T(8,128)(2,1)S(1)}, bf16[8,2560]{1,0:T(8,128)(2,1)S(1)}, u32[]{:S(2)}, u32[]{:S(2)}) collective-permute-start(bf16[8,2560]{1,0:T(8,128)(2,1)S(1)} %get-tuple-element.18), channel_id=1, source_target_pairs={{0,4},{4,8},{8,12},{12,0},{1,5},{5,9},{9,13},{13,1},{2,6},{6,10},{... | collective-permute-start | bytes 122888 | tf_op jit(solution)/shard_map/ppermute | solution.py:247
  4.5 2.6 %collective-permute-start.1 = (bf16[8,2560]{1,0:T(8,128)(2,1)S(1)}, bf16[8,2560]{1,0:T(8,128)(2,1)S(1)}, u32[]{:S(2)}, u32[]{:S(2)}) collective-permute-start(bf16[8,2560]{1,0:T(8,128)(2,1)S(1)} %get-tuple-element.19), channel_id=1, source_target_pairs={{0,8},{4,12},{8,0},{12,4},{1,9},{5,13},{9,1},{13,5},{2,10},{6,14},... | collective-permute-start | bytes 122888 | tf_op jit(solution)/shard_map/ppermute | solution.py:247
  7.0 1.3 %collective-permute-start.2 = (bf16[8,2560]{1,0:T(8,128)(2,1)S(1)}, bf16[8,2560]{1,0:T(8,128)(2,1)S(1)}, u32[]{:S(2)}, u32[]{:S(2)}) collective-permute-start(bf16[8,2560]{1,0:T(8,128)(2,1)S(1)} %get-tuple-element.20), channel_id=1, source_target_pairs={{0,12},{4,0},{8,4},{12,8},{1,13},{5,1},{9,5},{13,9},{2,14},{6,2},{... | collective-permute-start | bytes 122888 | tf_op jit(solution)/shard_map/ppermute | solution.py:247
  8.4 0.7 collective-permute-start.3
  9.1 0.3 collective-permute-start.4
  9.4 0.0 collective-permute-done.refs_1_
  9.4 2.8 %collective-permute-start.5 = (bf16[8,6912]{1,0:T(8,128)(2,1)S(1)}, bf16[8,6912]{1,0:T(8,128)(2,1)S(1)}, u32[]{:S(2)}, u32[]{:S(2)}) collective-permute-start(bf16[8,6912]{1,0:T(8,128)(2,1)S(1)} %get-tuple-element.24), channel_id=1, source_target_pairs={{0,12},{4,0},{8,4},{12,8},{1,13},{5,1},{9,5},{13,9},{2,14},{6,2},{... | collective-permute-start | bytes 331784 | tf_op jit(solution)/shard_map/ppermute | solution.py:247
  12.2 0.0 collective-permute-done.1.refs_2_
  12.2 0.0 collective-permute-done.2.refs_3_
  12.2 48.0 %shard_map.74.mapped_ref = f32[4,32,6912]{2,1,0:T(8,128)S(1)} custom-call(bf16[1,2560,6912]{2,1,0:T(8,128)(2,1)} %lam_ref.1, bf16[4,8,5120]{2,1,0:T(8,128)(2,1)} %left_ref.1, bf16[4,8,13824]{2,1,0:T(8,128)(2,1)} %right_ref.1, bf16[8,2560]{1,0:T(8,128)(2,1)S(1)} %get-tuple-element.17.refs_0_, bf16[8,2560]{1,0:T(8,128)(2,1)S(1)} %collective-permute-done.refs_1_, ...), custom_call_target="tpu_custom_call" | custom-call | flops 72477573120 | bytes 35389440 | tf_op jit(solution)/shard_map/pallas_call | solution.py:171
  60.2 0.0 collective-permute-done.3.refs_1_
  60.2 0.0 collective-permute-done.4.refs_2_
  60.3 0.0 collective-permute-done.5.refs_3_
  60.3 1.1 %shard_map.75 = (f32[2,4]{1,0:T(2,128)S(1)}, f32[2,4]{1,0:T(2,128)S(1)}, f32[2,4]{1,0:T(2,128)S(1)}, f32[2,4]{1,0:T(2,128)S(1)}) custom-call(s32[1,4]{1,0:T(1,128)} %live_ref.1, f32[4,32,6912]{2,1,0:T(8,128)S(1)} %shard_map.74.mapped_ref, bf16[8,6912]{1,0:T(8,128)(2,1)S(1)} %get-tuple-element.21.refs_0_, bf16[8,6912]{1,0:T(8,128)(2,1)S(1)} %collective-permute-done.3.refs_1_, ...), custom_call_target="tpu_custom_call" | custom-call | tf_op jit(solution)/shard_map/pallas_call | solution.py:232
  61.3 2.5 %collective-permute-start.6 = (f32[2,4]{1,0:T(2,128)S(1)}, f32[2,4]{1,0:T(2,128)S(1)}, u32[]{:S(2)}, u32[]{:S(2)}) collective-permute-start(f32[2,4]{1,0:T(2,128)S(1)} %get-tuple-element.26), channel_id=1, source_target_pairs={{0,12},{4,0},{8,4},{12,8},{1,13},{5,1},{9,5},{13,9},{2,14},{6,2},{... | collective-permute-start | bytes 104 | tf_op jit(solution)/shard_map/ppermute | solution.py:247
  63.9 0.0 collective-permute-start.7
  63.9 1.5 %collective-permute-start.8 = (f32[2,4]{1,0:T(2,128)S(1)}, f32[2,4]{1,0:T(2,128)S(1)}, u32[]{:S(2)}, u32[]{:S(2)}) collective-permute-start(f32[2,4]{1,0:T(2,128)S(1)} %get-tuple-element.28), channel_id=1, source_target_pairs={{0,4},{4,8},{8,12},{12,0},{1,5},{5,9},{9,13},{13,1},{2,6},{6,10},{... | collective-permute-start | bytes 104 | tf_op jit(solution)/shard_map/ppermute | solution.py:247
  65.4 0.0 collective-permute-done.6
  65.4 2.9 %collective-permute-done.7 = f32[2,4]{1,0:T(2,128)S(1)} collective-permute-done((f32[2,4]{1,0:T(2,128)S(1)}, f32[2,4]{1,0:T(2,128)S(1)}, u32[]{:S(2)}, u32[]{:S(2)}) %collective-permute-start.7) | collective-permute-done | bytes 64 | tf_op jit(solution)/shard_map/ppermute | solution.py:247
  68.4 0.9 %collective-permute-done.8 = f32[2,4]{1,0:T(2,128)S(1)} collective-permute-done((f32[2,4]{1,0:T(2,128)S(1)}, f32[2,4]{1,0:T(2,128)S(1)}, u32[]{:S(2)}, u32[]{:S(2)}) %collective-permute-start.8) | collective-permute-done | bytes 64 | tf_op jit(solution)/shard_map/ppermute | solution.py:247
  69.3 0.6 add_bitcast_fusion
Async XLA Ops:
  1.3 8.1 %collective-permute-start = (bf16[8,2560]{1,0:T(8,128)(2,1)S(1)}, bf16[8,2560]{1,0:T(8,128)(2,1)S(1)}, u32[]{:S(2)}, u32[]{:S(2)}) collective-permute-start(bf16[8,2560]{1,0:T(8,128)(2,1)S(1)} %get-tuple-element.18), channel_id=1, source_target_pairs={{0,4},{4,8},{8,12},{12,0},{1,5},{5,9},{9,13},{13,1},{2,6},{6,10},{... | collective-permute-start | bytes 122888 | tf_op jit(solution)/shard_map/ppermute | solution.py:247
  4.5 7.8 %collective-permute-start.1 = (bf16[8,2560]{1,0:T(8,128)(2,1)S(1)}, bf16[8,2560]{1,0:T(8,128)(2,1)S(1)}, u32[]{:S(2)}, u32[]{:S(2)}) collective-permute-start(bf16[8,2560]{1,0:T(8,128)(2,1)S(1)} %get-tuple-element.19), channel_id=1, source_target_pairs={{0,8},{4,12},{8,0},{12,4},{1,9},{5,13},{9,1},{13,5},{2,10},{6,14},... | collective-permute-start | bytes 122888 | tf_op jit(solution)/shard_map/ppermute | solution.py:247
  7.0 5.2 %collective-permute-start.2 = (bf16[8,2560]{1,0:T(8,128)(2,1)S(1)}, bf16[8,2560]{1,0:T(8,128)(2,1)S(1)}, u32[]{:S(2)}, u32[]{:S(2)}) collective-permute-start(bf16[8,2560]{1,0:T(8,128)(2,1)S(1)} %get-tuple-element.20), channel_id=1, source_target_pairs={{0,12},{4,0},{8,4},{12,8},{1,13},{5,1},{9,5},{13,9},{2,14},{6,2},{... | collective-permute-start | bytes 122888 | tf_op jit(solution)/shard_map/ppermute | solution.py:247
  8.4 51.8 %collective-permute-start.3 = (bf16[8,6912]{1,0:T(8,128)(2,1)S(1)}, bf16[8,6912]{1,0:T(8,128)(2,1)S(1)}, u32[]{:S(2)}, u32[]{:S(2)}) collective-permute-start(bf16[8,6912]{1,0:T(8,128)(2,1)S(1)} %get-tuple-element.22), channel_id=1, source_target_pairs={{0,4},{4,8},{8,12},{12,0},{1,5},{5,9},{9,13},{13,1},{2,6},{6,10},{... | collective-permute-start | bytes 331784 | tf_op jit(solution)/shard_map/ppermute | solution.py:247
  9.1 51.2 %collective-permute-start.4 = (bf16[8,6912]{1,0:T(8,128)(2,1)S(1)}, bf16[8,6912]{1,0:T(8,128)(2,1)S(1)}, u32[]{:S(2)}, u32[]{:S(2)}) collective-permute-start(bf16[8,6912]{1,0:T(8,128)(2,1)S(1)} %get-tuple-element.23), channel_id=1, source_target_pairs={{0,8},{4,12},{8,0},{12,4},{1,9},{5,13},{9,1},{13,5},{2,10},{6,14},... | collective-permute-start | bytes 331784 | tf_op jit(solution)/shard_map/ppermute | solution.py:247
  9.4 50.9 %collective-permute-start.5 = (bf16[8,6912]{1,0:T(8,128)(2,1)S(1)}, bf16[8,6912]{1,0:T(8,128)(2,1)S(1)}, u32[]{:S(2)}, u32[]{:S(2)}) collective-permute-start(bf16[8,6912]{1,0:T(8,128)(2,1)S(1)} %get-tuple-element.24), channel_id=1, source_target_pairs={{0,12},{4,0},{8,4},{12,8},{1,13},{5,1},{9,5},{13,9},{2,14},{6,2},{... | collective-permute-start | bytes 331784 | tf_op jit(solution)/shard_map/ppermute | solution.py:247
  61.3 4.1 %collective-permute-start.6 = (f32[2,4]{1,0:T(2,128)S(1)}, f32[2,4]{1,0:T(2,128)S(1)}, u32[]{:S(2)}, u32[]{:S(2)}) collective-permute-start(f32[2,4]{1,0:T(2,128)S(1)} %get-tuple-element.26), channel_id=1, source_target_pairs={{0,12},{4,0},{8,4},{12,8},{1,13},{5,1},{9,5},{13,9},{2,14},{6,2},{... | collective-permute-start | bytes 104 | tf_op jit(solution)/shard_map/ppermute | solution.py:247
  63.9 4.5 %collective-permute-start.7 = (f32[2,4]{1,0:T(2,128)S(1)}, f32[2,4]{1,0:T(2,128)S(1)}, u32[]{:S(2)}, u32[]{:S(2)}) collective-permute-start(f32[2,4]{1,0:T(2,128)S(1)} %get-tuple-element.27), channel_id=1, source_target_pairs={{0,8},{4,12},{8,0},{12,4},{1,9},{5,13},{9,1},{13,5},{2,10},{6,14},... | collective-permute-start | bytes 104 | tf_op jit(solution)/shard_map/ppermute | solution.py:247
  63.9 5.4 %collective-permute-start.8 = (f32[2,4]{1,0:T(2,128)S(1)}, f32[2,4]{1,0:T(2,128)S(1)}, u32[]{:S(2)}, u32[]{:S(2)}) collective-permute-start(f32[2,4]{1,0:T(2,128)S(1)} %get-tuple-element.28), channel_id=1, source_target_pairs={{0,4},{4,8},{8,12},{12,0},{1,5},{5,9},{9,13},{13,1},{2,6},{6,10},{... | collective-permute-start | bytes 104 | tf_op jit(solution)/shard_map/ppermute | solution.py:247
